TPU v7x, 32 devices: a whole 2x2x4 slice. The times are simulated.
32 devices in a mesh: energy: 4 (over x, core), slab: 8 (over z, y).
Axes of the slice: x: 2, y: 2, z: 4, core: 2. Of those that a mesh axis runs over, the one named last changes fastest.
Arguments:
- g_lesser: bfloat16 [4, 8, 3, 2, 256, 256], P('energy', 'slab'), may hold values from -6 to 6
- g_greater: bfloat16 [4, 8, 3, 2, 256, 256], P('energy', 'slab'), may hold values from -6 to 6
- v_diag: bfloat16 [8, 2, 256, 256], P('slab'), may hold values from -0.15625 to 0.15625
- v_upper: bfloat16 [8, 2, 256, 256], P('slab'), may hold values from -0.15625 to 0.15625
Outputs:
- w_diag: bfloat16 [4, 8, 2, 256, 256], P('energy', 'slab')
- w_upper: bfloat16 [4, 8, 2, 256, 256], P('energy', 'slab')
All inputs are finite; a program needn't handle non-finite values.
Results may differ from a plain program's by a relative error of at most 0.0058.
Values may be sent and summed in bfloat16 or wider, within the bound.
No kernel may reach another device: no remote copies, remote signals or barrier semaphores. Data moves between devices by JAX's collectives and lax.ppermute only.
A program may use at most 64 MiB of HBM per device.

v0:
```python
import math

import jax
import jax.numpy as jnp
from jax import lax
from jax.sharding import PartitionSpec as P


def extended(shard, sides, width):
    for axis, dim in sides:
        count, length = (lax.axis_size(axis), shard.shape[dim])
        up = [(i, (i + 1) % count) for i in range(count - 1)]
        down = [(j, i) for i, j in up]
        last = lax.slice_in_dim(shard, length - width, length, axis=dim)
        initial = lax.slice_in_dim(shard, 0, width, axis=dim)
        before = lax.ppermute(last, axis, up)
        after = lax.ppermute(initial, axis, down)
        shard = jnp.concatenate([before, shard, after], axis=dim)
    return shard


def passed_along(value, axis, steps):
    count = lax.axis_size(axis)
    initial, last = (max(0, -steps), min(count, count - steps))
    return lax.ppermute(value, axis, [(source, source + steps) for source in range(initial, last)])


def complex_product(left_block, right_block, left_adjoint=False, right_adjoint=False):
    left_re = left_block[..., 0, :, :]
    left_im = left_block[..., 1, :, :]
    right_re = right_block[..., 0, :, :]
    right_im = right_block[..., 1, :, :]
    pattern = (
        ("...ji" if left_adjoint else "...ij")
        + ","
        + ("...kj" if right_adjoint else "...jk")
        + "->...ik"
    )

    def contract(first_part, second_part):
        return jnp.einsum(pattern, first_part, second_part, preferred_element_type=jnp.float32)

    left_sign = -1.0 if left_adjoint else 1.0
    right_sign = -1.0 if right_adjoint else 1.0
    real_part = contract(left_re, right_re) - left_sign * right_sign * contract(left_im, right_im)
    imag_part = right_sign * contract(left_re, right_im) + left_sign * contract(left_im, right_re)
    return jnp.stack([real_part, imag_part], axis=-3)


def transform(table, signal):
    return jnp.einsum("fn,n...->f...", table, signal, precision=lax.Precision.HIGH)


def correlate(pieces):
    lesser, greater = pieces
    energies = lesser.shape[0]
    length = 2 * energies
    frequency = jnp.arange(length, dtype=jnp.int32)
    energy_ids = jnp.arange(energies, dtype=jnp.int32)
    step_angle = 2.0 * math.pi / length
    forward_angle = (frequency[:, None] * energy_ids[None, :] % length).astype(
        jnp.float32
    ) * step_angle
    shifts = energy_ids - energies // 2
    inverse_angle = (shifts[:, None] * frequency[None, :] % length).astype(jnp.float32) * step_angle
    forward_cos = jnp.cos(forward_angle)
    forward_sin = jnp.sin(forward_angle)
    inverse_cos = jnp.cos(inverse_angle)
    inverse_sin = jnp.sin(inverse_angle)

    def spectrum(signal):
        signal_re = signal[:, :, :, 0].astype(jnp.float32)
        signal_im = signal[:, :, :, 1].astype(jnp.float32)
        spec_re = transform(forward_cos, signal_re) + transform(forward_sin, signal_im)
        spec_im = transform(forward_cos, signal_im) - transform(forward_sin, signal_re)
        return (spec_re, spec_im)

    lesser_re, lesser_im = spectrum(lesser)
    greater_re, greater_im = spectrum(greater)
    cross_re = lesser_re * greater_re + lesser_im * greater_im
    cross_im = lesser_im * greater_re - lesser_re * greater_im
    corr_re = (transform(inverse_cos, cross_re) - transform(inverse_sin, cross_im)) / length
    corr_im = (transform(inverse_cos, cross_im) + transform(inverse_sin, cross_re)) / length
    factor = 1.0 / math.sqrt(energies)
    polar_entries = jnp.stack([-corr_im * factor, corr_re * factor], axis=3).astype(jnp.bfloat16)
    return lax.all_to_all(polar_entries, "energy", split_axis=0, concat_axis=4, tiled=True)


def per_device(g_lesser, g_greater, v_diag, v_upper):
    local_rows = v_diag.shape[0]
    total_rows = local_rows * lax.axis_size("slab")
    first_row = lax.axis_index("slab") * local_rows
    inside = first_row + jnp.arange(local_rows, dtype=jnp.int32) < total_rows - 1
    inside = inside.astype(jnp.bfloat16)[:, None, None, None]
    coupling = jnp.stack([v_diag, v_upper * inside], axis=1)
    padded = extended(coupling, (("slab", 0),), 1)
    diag_below = padded[:-2, 0][None]
    diag_middle = padded[1:-1, 0][None]
    diag_above = padded[2:, 0][None]
    upper_below = padded[:-2, 1][None]
    upper_middle = padded[1:-1, 1][None]
    upper_above = padded[2:, 1][None]
    middle = correlate(
        (
            lax.all_to_all(g_lesser, "energy", split_axis=4, concat_axis=0, tiled=True),
            lax.all_to_all(g_greater, "energy", split_axis=4, concat_axis=0, tiled=True),
        )
    )
    toward_above_y = complex_product(middle[:, :, 1], upper_middle) + complex_product(
        middle[:, :, 2], diag_above
    )
    toward_above_z = complex_product(middle[:, :, 2], upper_above)
    toward_below_y = complex_product(middle[:, :, 0], diag_below) + complex_product(
        middle[:, :, 1], upper_below, False, True
    )
    toward_below_z = (
        complex_product(middle[:, :, 0], upper_below)
        + complex_product(middle[:, :, 1], diag_middle)
        + complex_product(middle[:, :, 2], upper_middle, False, True)
    )
    sent_up = jnp.stack([toward_above_y, toward_above_z], axis=2).astype(jnp.bfloat16)
    sent_down = jnp.stack([toward_below_y, toward_below_z], axis=2).astype(jnp.bfloat16)
    arrived_below = passed_along(sent_up[:, -1:], "slab", 1)
    from_below = jnp.concatenate([arrived_below, sent_up[:, :-1]], axis=1)
    arrived_above = passed_along(sent_down[:, :1], "slab", -1)
    from_above = jnp.concatenate([sent_down[:, 1:], arrived_above], axis=1)
    below_y = from_below[:, :, 0]
    below_z = from_below[:, :, 1]
    above_y = from_above[:, :, 0]
    above_z = from_above[:, :, 1]
    middle_y = (
        complex_product(middle[:, :, 0], upper_below)
        + complex_product(middle[:, :, 1], diag_middle)
        + complex_product(middle[:, :, 2], upper_middle, False, True)
    ).astype(jnp.bfloat16)
    middle_z = (
        complex_product(middle[:, :, 1], upper_middle)
        + complex_product(middle[:, :, 2], diag_above)
    ).astype(jnp.bfloat16)
    w_diag = (
        complex_product(upper_below, below_y, True, False)
        + complex_product(diag_middle, middle_y)
        + complex_product(upper_middle, above_y)
    ).astype(jnp.bfloat16)
    w_upper = (
        complex_product(upper_below, below_z, True, False)
        + complex_product(diag_middle, middle_z)
        + complex_product(upper_middle, above_z)
    ).astype(jnp.bfloat16)
    return (w_diag, w_upper)


def solution(mesh):
    placed = (
        P("energy", "slab", None, None, None, None),
        P("energy", "slab", None, None, None, None),
        P("slab", None, None, None),
        P("slab", None, None, None),
    )
    return jax.shard_map(
        per_device,
        mesh=mesh,
        in_specs=placed,
        out_specs=(P("energy", "slab", None, None, None), P("energy", "slab", None, None, None)),
        check_vma=False,
    )
```

profile of v0, /device:TPU:26, one launch (start us, length us, event | category | flops | bytes accessed | tf_op | source)
XLA Modules:
  0.0 119.2 jit_solution(980924947038684042)
XLA Ops:
  0.6 2.9 %copy.44 = bf16[1,1,3,2,256,256]{5,2,3,1,0,4:T(4,128)(2,1)} copy(bf16[1,1,3,2,256,256]{5,4,3,2,1,0:T(8,128)(2,1)} %param.5) | data formatting | bytes 1572864 | tf_op args[1]
  3.5 4.0 %all-to-all-start.1 = ((bf16[1,1,3,2,256,256]{5,2,3,1,0,4:T(4,128)(2,1)}), bf16[1,1,3,2,256,256]{5,2,3,1,0,4:T(4,128)(2,1)S(1)}, u32[]{:S(2)}, u32[]{:S(2)}) async-start(bf16[1,1,3,2,256,256]{5,2,3,1,0,4:T(4,128)(2,1)} %copy.44), calls=%async_computation.1 | async-start | bytes 2097152 | tf_op jit(solution)/shard_map/all_to_all | solution.py:106
  7.5 1.7 %copy.41 = bf16[1,1,3,2,256,256]{5,2,3,1,0,4:T(4,128)(2,1)} copy(bf16[1,1,3,2,256,256]{5,4,3,2,1,0:T(8,128)(2,1)S(1)} %copy-done.2) | data formatting | bytes 1572864 | tf_op args[0]
  9.2 11.1 %all-to-all-done.1 = bf16[1,1,3,2,256,256]{5,2,3,1,0,4:T(4,128)(2,1)S(1)} async-done(((bf16[1,1,3,2,256,256]{5,2,3,1,0,4:T(4,128)(2,1)}), bf16[1,1,3,2,256,256]{5,2,3,1,0,4:T(4,128)(2,1)S(1)}, u32[]{:S(2)}, u32[]{:S(2)}) %all-to-all-start.1) | async-done | bytes 786464 | tf_op jit(solution)/shard_map/all_to_all | solution.py:106
  20.3 5.1 %all-to-all-start = ((bf16[1,1,3,2,256,256]{5,2,3,1,0,4:T(4,128)(2,1)}), bf16[1,1,3,2,256,256]{5,2,3,1,0,4:T(4,128)(2,1)S(1)}, u32[]{:S(2)}, u32[]{:S(2)}) async-start(bf16[1,1,3,2,256,256]{5,2,3,1,0,4:T(4,128)(2,1)} %copy.41), calls=%async_computation | async-start | bytes 2097152 | tf_op jit(solution)/shard_map/all_to_all | solution.py:105
  25.4 0.7 copy.75
  26.2 1.9 %fusion.43 = f32[8,3,64,256]{3,0,2,1:T(8,128)} fusion(bf16[4,1,3,2,64,256]{5,0,4,2,3,1:T(4,128)(2,1)S(1)} %bitcast.359), kind=kOutput, calls=%fused_computation.102 | convolution fusion | flops 9437632 | bytes 1966080 | tf_op jit(solution)/shard_map/fn,n...->f.../dot_general | solution.py:51
  28.1 0.7 fusion.44
  28.8 9.4 %all-to-all-done = bf16[1,1,3,2,256,256]{5,2,3,1,0,4:T(4,128)(2,1)S(1)} async-done(((bf16[1,1,3,2,256,256]{5,2,3,1,0,4:T(4,128)(2,1)}), bf16[1,1,3,2,256,256]{5,2,3,1,0,4:T(4,128)(2,1)S(1)}, u32[]{:S(2)}, u32[]{:S(2)}) %all-to-all-start) | async-done | bytes 786464 | tf_op jit(solution)/shard_map/all_to_all | solution.py:105
  38.2 0.7 copy.76
  39.0 0.7 fusion.41
  39.8 0.7 fusion.42
  40.5 0.8 convolution_add_fusion.1
  41.3 0.8 convolution_subtract_fusion.1
  42.1 0.8 convolution_subtract_fusion
  42.9 1.2 %multiply_subtract_fusion = (f32[8,3,64,256]{3,0,2,1:T(8,128)S(1)}, f32[8,3,64,256]{3,0,2,1:T(8,128)S(1)}) fusion(f32[8,3,64,256]{3,0,2,1:T(8,128)S(1)} %convolution_subtract_fusion, f32[8,3,64,256]{3,0,2,1:T(8,128)S(1)} %convolution_subtract_fusion.1, f32[8,3,64,256]{3,0,2,1:T(8,128)S(1)} %convolution_add_fusion.1, f32[8,3,64,256]{3,0,2,1:T(8,128)S(1)} %fusion.42, ...), kind=kOutput, calls=%fused_computation.1 | convolution fusion | flops 12190144 | bytes 9830400 | tf_op jit(solution)/shard_map/fn,n...->f.../dot_general | solution.py:51
  44.1 0.9 fusion.80
  45.0 0.9 fusion.78
  45.9 1.1 fusion.7
  46.9 1.0 fusion.6
  47.9 0.6 pad_maximum_fusion
  48.5 1.0 copy.47
  49.6 5.1 %all-to-all-start.2 = ((bf16[4,1,3,2,64,256]{5,4,2,3,1,0:T(8,128)(2,1)}), bf16[4,1,3,2,64,256]{5,4,2,3,1,0:T(8,128)(2,1)S(1)}, u32[]{:S(2)}, u32[]{:S(2)}) async-start(bf16[4,1,3,2,64,256]{5,4,2,3,1,0:T(8,128)(2,1)} %copy.47), calls=%async_computation.2 | async-start | bytes 1572864 | tf_op jit(solution)/shard_map/all_to_all | solution.py:86
  54.8 3.6 %collective-permute-start = (bf16[1,2,2,256,256]{4,3,2,1,0:T(8,128)(2,1)S(1)}, bf16[1,2,2,256,256]{4,3,2,1,0:T(8,128)(2,1)S(1)}, u32[]{:S(2)}, u32[]{:S(2)}) collective-permute-start(bf16[1,2,2,256,256]{4,3,2,1,0:T(8,128)(2,1)S(1)} %pad_maximum_fusion.1), channel_id=1, source_target_pairs={{0,1},{1,2},{2,3},{3,4},{4,5},{5,6},{6,7},{8,9},{9,10},{10,11},{11... | collective-permute-start | bytes 1572872 | tf_op jit(solution)/shard_map/ppermute | solution.py:16
  58.4 3.3 %collective-permute-start.1 = (bf16[1,2,2,256,256]{4,3,2,1,0:T(8,128)(2,1)S(1)}, bf16[1,2,2,256,256]{4,3,2,1,0:T(8,128)(2,1)S(1)}, u32[]{:S(2)}, u32[]{:S(2)}) collective-permute-start(bf16[1,2,2,256,256]{4,3,2,1,0:T(8,128)(2,1)S(1)} %pad_maximum_fusion.1), channel_id=1, source_target_pairs={{1,0},{2,1},{3,2},{4,3},{5,4},{6,5},{7,6},{9,8},{10,9},{11,10},{12... | collective-permute-start | bytes 1572872 | tf_op jit(solution)/shard_map/ppermute | solution.py:17
  61.7 3.0 %all-to-all-done.2 = bf16[4,1,3,2,64,256]{5,4,2,3,1,0:T(8,128)(2,1)S(1)} async-done(((bf16[4,1,3,2,64,256]{5,4,2,3,1,0:T(8,128)(2,1)}), bf16[4,1,3,2,64,256]{5,4,2,3,1,0:T(8,128)(2,1)S(1)}, u32[]{:S(2)}, u32[]{:S(2)}) %all-to-all-start.2) | async-done | bytes 786464 | tf_op jit(solution)/shard_map/all_to_all | solution.py:86
  64.8 0.2 fusion.69
  65.0 0.2 convolution_multiply_fusion.4
  65.8 0.2 fusion.23
  66.0 0.2 convolution_add_fusion.9
  66.8 15.9 %collective-permute-done.1 = bf16[1,2,2,256,256]{4,3,2,1,0:T(8,128)(2,1)S(1)} collective-permute-done((bf16[1,2,2,256,256]{4,3,2,1,0:T(8,128)(2,1)S(1)}, bf16[1,2,2,256,256]{4,3,2,1,0:T(8,128)(2,1)S(1)}, u32[]{:S(2)}, u32[]{:S(2)}) %collective-permute-start.1) | collective-permute-done | bytes 524320 | tf_op jit(solution)/shard_map/ppermute | solution.py:17
  84.7 0.2 convolution_multiply_fusion.3
  85.0 0.2 fusion.68
  86.0 0.2 fusion.20
  86.2 0.2 fusion.19
  87.1 1.9 %collective-permute-start.3 = (bf16[1,1,2,2,256,256]{5,4,3,2,1,0:T(8,128)(2,1)S(1)}, bf16[1,1,2,2,256,256]{5,4,3,2,1,0:T(8,128)(2,1)S(1)}, u32[]{:S(2)}, u32[]{:S(2)}) collective-permute-start(bf16[1,1,2,2,256,256]{5,4,3,2,1,0:T(8,128)(2,1)S(1)} %pad_maximum_fusion.3), channel_id=1, source_target_pairs={{1,0},{2,1},{3,2},{4,3},{5,4},{6,5},{7,6},{9,8},{10,9},{11,10},{12... | collective-permute-start | bytes 1572872 | tf_op jit(solution)/shard_map/ppermute | solution.py:25
  90.3 3.9 %collective-permute-start.2 = (bf16[1,1,2,2,256,256]{5,4,3,2,1,0:T(8,128)(2,1)S(1)}, bf16[1,1,2,2,256,256]{5,4,3,2,1,0:T(8,128)(2,1)S(1)}, u32[]{:S(2)}, u32[]{:S(2)}) collective-permute-start(bf16[1,1,2,2,256,256]{5,4,3,2,1,0:T(8,128)(2,1)S(1)} %pad_maximum_fusion.2), channel_id=1, source_target_pairs={{0,1},{1,2},{2,3},{3,4},{4,5},{5,6},{6,7},{8,9},{9,10},{10,11},{11... | collective-permute-start | bytes 1572872 | tf_op jit(solution)/shard_map/ppermute | solution.py:25
  95.2 18.9 %collective-permute-done.3 = bf16[1,1,2,2,256,256]{5,4,3,2,1,0:T(8,128)(2,1)S(1)} collective-permute-done((bf16[1,1,2,2,256,256]{5,4,3,2,1,0:T(8,128)(2,1)S(1)}, bf16[1,1,2,2,256,256]{5,4,3,2,1,0:T(8,128)(2,1)S(1)}, u32[]{:S(2)}, u32[]{:S(2)}) %collective-permute-start.3) | collective-permute-done | bytes 524320 | tf_op jit(solution)/shard_map/ppermute | solution.py:25
  115.7 0.2 convolution_multiply_fusion.1
  116.0 0.2 convolution_multiply_fusion
  116.2 0.2 fusion.15
  116.4 0.2 fusion.14
  116.7 0.8 fusion.39
  117.5 0.2 convolution_multiply_fusion.7
  117.7 0.2 convolution_multiply_fusion.6
  117.9 0.2 fusion.25
  118.1 0.2 fusion.24
  118.4 0.8 fusion.32
  (64 shorter events, 8.3 us)
Async XLA Ops:
  0.6 6.9 %copy-start.2 = (bf16[1,1,3,2,256,256]{5,4,3,2,1,0:T(8,128)(2,1)S(1)}, bf16[1,1,3,2,256,256]{5,4,3,2,1,0:T(8,128)(2,1)}, u32[]{:S(2)}) copy-start(bf16[1,1,3,2,256,256]{5,4,3,2,1,0:T(8,128)(2,1)} %param.4) | copy-start | bytes 2359300
  3.5 16.8 %all-to-all-start.1 = ((bf16[1,1,3,2,256,256]{5,2,3,1,0,4:T(4,128)(2,1)}), bf16[1,1,3,2,256,256]{5,2,3,1,0,4:T(4,128)(2,1)S(1)}, u32[]{:S(2)}, u32[]{:S(2)}) async-start(bf16[1,1,3,2,256,256]{5,2,3,1,0,4:T(4,128)(2,1)} %copy.44), calls=%async_computation.1 | async-start | bytes 2097152 | tf_op jit(solution)/shard_map/all_to_all | solution.py:106
  20.3 17.9 %all-to-all-start = ((bf16[1,1,3,2,256,256]{5,2,3,1,0,4:T(4,128)(2,1)}), bf16[1,1,3,2,256,256]{5,2,3,1,0,4:T(4,128)(2,1)S(1)}, u32[]{:S(2)}, u32[]{:S(2)}) async-start(bf16[1,1,3,2,256,256]{5,2,3,1,0,4:T(4,128)(2,1)} %copy.41), calls=%async_computation | async-start | bytes 2097152 | tf_op jit(solution)/shard_map/all_to_all | solution.py:105
  39.0 1.5 %copy-start.1 = (f32[8,3,64,256]{3,0,2,1:T(8,128)S(1)}, f32[8,3,64,256]{3,0,2,1:T(8,128)}, u32[]{:S(2)}) copy-start(f32[8,3,64,256]{3,0,2,1:T(8,128)} %fusion.43) | copy-start | bytes 4718596
  48.5 6.2 %copy-start.3 = (bf16[1,2,256,256]{3,2,1,0:T(8,128)(2,1)S(1)}, bf16[1,2,256,256]{3,2,1,0:T(8,128)(2,1)}, u32[]{:S(2)}) copy-start(bf16[1,2,256,256]{3,2,1,0:T(8,128)(2,1)} %param.7) | copy-start | bytes 786436
  48.5 6.2 %copy-start = (bf16[1,2,256,256]{3,2,1,0:T(8,128)(2,1)S(1)}, bf16[1,2,256,256]{3,2,1,0:T(8,128)(2,1)}, u32[]{:S(2)}) copy-start(bf16[1,2,256,256]{3,2,1,0:T(8,128)(2,1)} %param.6) | copy-start | bytes 786436
  49.6 15.1 %all-to-all-start.2 = ((bf16[4,1,3,2,64,256]{5,4,2,3,1,0:T(8,128)(2,1)}), bf16[4,1,3,2,64,256]{5,4,2,3,1,0:T(8,128)(2,1)S(1)}, u32[]{:S(2)}, u32[]{:S(2)}) async-start(bf16[4,1,3,2,64,256]{5,4,2,3,1,0:T(8,128)(2,1)} %copy.47), calls=%async_computation.2 | async-start | bytes 1572864 | tf_op jit(solution)/shard_map/all_to_all | solution.py:86
  54.8 29.6 %collective-permute-start = (bf16[1,2,2,256,256]{4,3,2,1,0:T(8,128)(2,1)S(1)}, bf16[1,2,2,256,256]{4,3,2,1,0:T(8,128)(2,1)S(1)}, u32[]{:S(2)}, u32[]{:S(2)}) collective-permute-start(bf16[1,2,2,256,256]{4,3,2,1,0:T(8,128)(2,1)S(1)} %pad_maximum_fusion.1), channel_id=1, source_target_pairs={{0,1},{1,2},{2,3},{3,4},{4,5},{5,6},{6,7},{8,9},{9,10},{10,11},{11... | collective-permute-start | bytes 1572872 | tf_op jit(solution)/shard_map/ppermute | solution.py:16
  58.4 24.4 %collective-permute-start.1 = (bf16[1,2,2,256,256]{4,3,2,1,0:T(8,128)(2,1)S(1)}, bf16[1,2,2,256,256]{4,3,2,1,0:T(8,128)(2,1)S(1)}, u32[]{:S(2)}, u32[]{:S(2)}) collective-permute-start(bf16[1,2,2,256,256]{4,3,2,1,0:T(8,128)(2,1)S(1)} %pad_maximum_fusion.1), channel_id=1, source_target_pairs={{1,0},{2,1},{3,2},{4,3},{5,4},{6,5},{7,6},{9,8},{10,9},{11,10},{12... | collective-permute-start | bytes 1572872 | tf_op jit(solution)/shard_map/ppermute | solution.py:17
  87.1 27.0 %collective-permute-start.3 = (bf16[1,1,2,2,256,256]{5,4,3,2,1,0:T(8,128)(2,1)S(1)}, bf16[1,1,2,2,256,256]{5,4,3,2,1,0:T(8,128)(2,1)S(1)}, u32[]{:S(2)}, u32[]{:S(2)}) collective-permute-start(bf16[1,1,2,2,256,256]{5,4,3,2,1,0:T(8,128)(2,1)S(1)} %pad_maximum_fusion.3), channel_id=1, source_target_pairs={{1,0},{2,1},{3,2},{4,3},{5,4},{6,5},{7,6},{9,8},{10,9},{11,10},{12... | collective-permute-start | bytes 1572872 | tf_op jit(solution)/shard_map/ppermute | solution.py:25
  90.3 25.3 %collective-permute-start.2 = (bf16[1,1,2,2,256,256]{5,4,3,2,1,0:T(8,128)(2,1)S(1)}, bf16[1,1,2,2,256,256]{5,4,3,2,1,0:T(8,128)(2,1)S(1)}, u32[]{:S(2)}, u32[]{:S(2)}) collective-permute-start(bf16[1,1,2,2,256,256]{5,4,3,2,1,0:T(8,128)(2,1)S(1)} %pad_maximum_fusion.2), channel_id=1, source_target_pairs={{0,1},{1,2},{2,3},{3,4},{4,5},{5,6},{6,7},{8,9},{9,10},{10,11},{11... | collective-permute-start | bytes 1572872 | tf_op jit(solution)/shard_map/ppermute | solution.py:25
where the time goes:
time: 120 us; the launch traced here: 119 us
  waiting for transfers between devices  58.3 us (49%)
  starting transfers between devices  27 us (22%)
  matrix products  22.5 us (19%)
  local copies, waits for them, and re-layouts  7.24 us (6%)
  other arithmetic  2.8 us (2%)
  between operations  1.33 us (1%)
    ppermute x2, waiting for transfers between devices, passed_along(): lax.ppermute(value, axis, [(source, source + steps) for source in range(i...  18.9 us
    ppermute x1, waiting for transfers between devices, extended(): after = lax.ppermute(initial, axis, down)  15.9 us
    dot_general x12, matrix products, transform(): jnp.einsum('fn,n...->f...', table, signal, precision=lax.Precision.HIGH)  11.5 us
    all_to_all x1, waiting for transfers between devices, per_device(): lax.all_to_all(g_greater, 'energy', split_axis=4, concat_axis=0, tiled=True)  11.1 us
    dot_general x56, matrix products, contract(): jnp.einsum(pattern, first_part, second_part, preferred_element_type=jnp.f...  11 us
    all_to_all x1, waiting for transfers between devices, per_device(): lax.all_to_all(g_lesser, 'energy', split_axis=4, concat_axis=0, tiled=True)  9.39 us
    ppermute x2, starting transfers between devices, passed_along(): lax.ppermute(value, axis, [(source, source + steps) for source in range(i...  5.87 us
    all_to_all x1, starting transfers between devices, per_device(): lax.all_to_all(g_lesser, 'energy', split_axis=4, concat_axis=0, tiled=True)  5.12 us
  transfers between devices with their start and end apart: 7, of which 5 were waited for; matrix products, arithmetic and copies ran while one was open for 10% of the time, Pallas kernels for 0%

commit v1 on v0

--- a/solution.py
+++ b/solution.py
@@ -3,6 +3,8 @@
 import jax
 import jax.numpy as jnp
 from jax import lax
+from jax.experimental import pallas as pl
+from jax.experimental.pallas import tpu as pltpu
 from jax.sharding import PartitionSpec as P
 
 
@@ -86,7 +88,7 @@
     return lax.all_to_all(polar_entries, "energy", split_axis=0, concat_axis=4, tiled=True)
 
 
-def per_device(g_lesser, g_greater, v_diag, v_upper):
+def general(g_lesser, g_greater, v_diag, v_upper):
     local_rows = v_diag.shape[0]
     total_rows = local_rows * lax.axis_size("slab")
     first_row = lax.axis_index("slab") * local_rows
@@ -150,6 +152,329 @@
     return (w_diag, w_upper)
 
 
+ON_CHIP = [(0, 1), (1, 0), (2, 3), (3, 2)]
+RAW = [(2, 0), (3, 1)]
+RAW_ONE = [(3, 1)]
+PARTIAL = [(0, 2), (1, 3)]
+
+
+def chunks_of(rows):
+    if rows % 256:
+        return ((0, rows),)
+    unit = rows // 16
+    sizes = (6 * unit, 5 * unit, 5 * unit)
+    starts = (0, 6 * unit, 11 * unit)
+    return tuple(zip(starts, sizes))
+
+
+def whole(shape):
+    return pl.BlockSpec(shape, lambda *_: (0,) * len(shape))
+
+
+def rows_of(shape, start, size):
+    block = tuple(pl.Element(size if at == 4 else n) for at, n in enumerate(shape))
+    return pl.BlockSpec(block, lambda *_: (0, 0, 0, 0, start, 0))
+
+
+def scalars():
+    return pl.BlockSpec(memory_space=pltpu.SMEM)
+
+
+def params():
+    return pltpu.CompilerParams(vmem_limit_bytes=48 << 20)
+
+
+def f32(value):
+    return value.astype(jnp.float32)
+
+
+def times_conj(left, right):
+    left_re, left_im = f32(left[0]), f32(left[1])
+    right_re, right_im = f32(right[0]), f32(right[1])
+    return (left_re * right_re + left_im * right_im, left_im * right_re - left_re * right_im)
+
+
+def added(first, second):
+    return (first[0] + second[0], first[1] + second[1])
+
+
+def partial_kernel(place, l_own, g_own, l_mate, g_mate, l_far, out):
+    l_own, g_own, l_mate, g_mate = (r.at[0, 0] for r in (l_own, g_own, l_mate, g_mate))
+    bands = l_own.shape[0]
+
+    @pl.when(place[0] == 0)
+    def _():
+        for b in range(bands):
+            total = added(times_conj(l_own[b], g_own[b]), times_conj(l_mate[b], g_mate[b]))
+            out[b, 0] = total[0].astype(out.dtype)
+            out[b, 1] = total[1].astype(out.dtype)
+
+    @pl.when(place[0] == 1)
+    def _():
+        for b in range(bands):
+            total = added(times_conj(l_own[b], g_mate[b]), times_conj(l_far[b], g_own[b]))
+            out[b, 0] = total[0].astype(out.dtype)
+            out[b, 1] = total[1].astype(out.dtype)
+
+
+def polar_kernel(factor, place, l_own, g_own, l_mate, g_mate, g_far, g_far_mate, l_far, arrived,
+                 w_m1, w_0, w_1, w_2, near, far, own, polar):
+    l_own, g_own, l_mate, g_mate = (r.at[0, 0] for r in (l_own, g_own, l_mate, g_mate))
+    bands, _, rows, width = l_own.shape
+
+    def put(b, total):
+        re = (-total[1] * factor).astype(polar.dtype)
+        im = (total[0] * factor).astype(polar.dtype)
+        polar[b, :rows, :width] = re
+        polar[b, rows:, :width] = im
+        polar[b, :rows, width:] = -im
+        polar[b, rows:, width:] = re
+
+    @pl.when(place[0] == 0)
+    def _():
+        for b in range(bands):
+            put(b, added(times_conj(l_own[b], g_far[b]), times_conj(l_mate[b], g_far_mate[b])))
+
+    @pl.when(place[0] == 1)
+    def _():
+        for b in range(bands):
+            total = added(times_conj(l_mate[b], g_own[b]), times_conj(l_own[b], g_far_mate[b]))
+            put(b, added(total, times_conj(l_far[b], g_far[b])))
+
+    @pl.when(place[0] == 2)
+    def _():
+        for b in range(bands):
+            total = added(times_conj(l_own[b], g_own[b]), times_conj(l_mate[b], g_mate[b]))
+            put(b, added(total, (f32(arrived[b, 0]), f32(arrived[b, 1]))))
+
+    @pl.when(place[0] == 3)
+    def _():
+        for b in range(bands):
+            total = times_conj(l_own[b], g_mate[b])
+            put(b, added(total, (f32(arrived[b, 0]), f32(arrived[b, 1]))))
+
+    def product(bands_used, weights):
+        total = None
+        for at, b in enumerate(bands_used):
+            term = jnp.dot(
+                polar[b],
+                weights[at * 2 * width : (at + 1) * 2 * width, :],
+                preferred_element_type=jnp.float32,
+            )
+            total = term if total is None else total + term
+        return total.astype(near.dtype).reshape(2, rows, width)
+
+    t_0 = product((0, 1, 2), w_0)
+    t_1 = product((1, 2), w_1)
+    t_m1 = product((0, 1), w_m1)
+    t_2 = product((2,), w_2)
+    own[0] = t_0
+    own[1] = t_1
+
+    @pl.when(place[1] == 0)
+    def _():
+        near[0] = t_1
+        near[1] = t_2
+        far[0] = t_m1
+        far[1] = t_0
+
+    @pl.when(place[1] == 1)
+    def _():
+        near[0] = t_m1
+        near[1] = t_0
+        far[0] = t_1
+        far[1] = t_2
+
+
+def coupling_kernel(place, diag, upper, near, near_mate, far, far_mate,
+                    w_m1, w_0, w_1, w_2, left):
+    width = diag.shape[-1]
+    core = place[2]
+    even = place[1] == 0
+
+    def adjoint(block):
+        return (block[0].T, -(block[1].T))
+
+    def put(target, at, block):
+        target[at * 2 * width : at * 2 * width + width, :] = block[0]
+        target[at * 2 * width + width : (at + 1) * 2 * width, :] = block[1]
+
+    def put_left(at, block):
+        base = at * 2 * width
+        left[:width, base : base + width] = block[0]
+        left[width:, base : base + width] = block[1]
+        left[:width, base + width : base + 2 * width] = -block[1]
+        left[width:, base + width : base + 2 * width] = block[0]
+
+    def work(diag_near, upper_near, diag_far, upper_far):
+        own = (upper[0], upper[1])
+        own_adjoint = adjoint(own)
+        put(w_0, 1, diag)
+        put(w_0, 2, own_adjoint)
+        put(w_1, 0, own)
+        put_left(1, (diag[0], diag[1]))
+
+        def sided(diag_below, upper_below, diag_above, upper_above, below_at, above_at):
+            below = (upper_below[0], upper_below[1])
+            below_adjoint = adjoint(below)
+            put(w_m1, 0, diag_below)
+            put(w_m1, 1, below_adjoint)
+            put(w_0, 0, below)
+            put(w_1, 1, diag_above)
+            put(w_2, 0, upper_above)
+            put_left(below_at, below_adjoint)
+            put_left(above_at, own)
+
+        @pl.when(even)
+        def _():
+            sided(diag_far, upper_far, diag_near, upper_near, 2, 0)
+
+        @pl.when(jnp.logical_not(even))
+        def _():
+            sided(diag_near, upper_near, diag_far, upper_far, 0, 2)
+
+    @pl.when(core == 0)
+    def _():
+        work(near, near_mate, far, far_mate)
+
+    @pl.when(core == 1)
+    def _():
+        work(near_mate, near, far_mate, far)
+
+
+def final_kernel(count, *refs):
+    own, near, far = refs[:count], refs[count : 2 * count], refs[2 * count : 3 * count]
+    left, w_diag, w_upper, gathered, sems = refs[3 * count :]
+    width = w_diag.shape[-1]
+    copies = []
+    for place, group in enumerate((near, own, far)):
+        start = 0
+        for at, piece in enumerate(group):
+            size = piece.shape[2]
+            copy = pltpu.make_async_copy(
+                piece,
+                gathered.at[place, :, :, start : start + size],
+                sems.at[place, at],
+            )
+            copy.start()
+            copies.append(copy)
+            start += size
+    for copy in copies:
+        copy.wait()
+    for index, out in enumerate((w_diag, w_upper)):
+        total = None
+        for place in range(3):
+            term = jnp.dot(
+                left[:, place * 2 * width : (place + 1) * 2 * width],
+                gathered[place, index].reshape(2 * width, width),
+                preferred_element_type=jnp.float32,
+            )
+            total = term if total is None else total + term
+        out[...] = total.astype(out.dtype).reshape(2, width, width)
+
+
+def exchanged(g_lesser, g_greater, v_diag, v_upper):
+    bf16 = jnp.bfloat16
+    energies = lax.axis_size("energy")
+    slabs = lax.axis_size("slab")
+    bands, width = g_lesser.shape[2], g_lesser.shape[5]
+    energy = lax.axis_index("energy")
+    slab = lax.axis_index("slab")
+    core = energy % 2
+    place = jnp.stack([energy, slab % 2, core]).astype(jnp.int32)
+    near_pairs = [(i, i ^ 1) for i in range(slabs)]
+    far_pairs = [(i, i + 1) for i in range(1, slabs - 1, 2)]
+    far_pairs = far_pairs + [(j, i) for i, j in far_pairs]
+
+    l_own, g_own = g_lesser, g_greater
+    l_mate = lax.ppermute(l_own, "energy", ON_CHIP)
+    g_mate = lax.ppermute(g_own, "energy", ON_CHIP)
+
+    upper = jnp.where(slab == slabs - 1, jnp.zeros_like(v_upper), v_upper)[0]
+    diag = v_diag[0]
+    sent = jnp.where(core == 0, diag, upper)
+    v_near = lax.ppermute(sent, "slab", near_pairs)
+    v_far = lax.ppermute(sent, "slab", far_pairs)
+    v_near_mate = lax.ppermute(v_near, "energy", ON_CHIP)
+    v_far_mate = lax.ppermute(v_far, "energy", ON_CHIP)
+    square = (2, width, width)
+    right = [
+        jax.ShapeDtypeStruct((2 * width * n, width), bf16) for n in (2, 3, 2, 1)
+    ]
+    *rights, left = pl.pallas_call(
+        coupling_kernel,
+        out_shape=(*right, jax.ShapeDtypeStruct((2 * width, 6 * width), bf16)),
+        in_specs=[scalars()] + [whole(square)] * 6,
+        out_specs=tuple(whole(r.shape) for r in right) + (whole((2 * width, 6 * width)),),
+        compiler_params=params(),
+        grid=(1,),
+        name="coupling",
+    )(place, diag, upper, v_near, v_near_mate, v_far, v_far_mate)
+
+    owns, nears, fars = [], [], []
+    for start, size in chunks_of(width):
+        def cut(value):
+            return lax.slice_in_dim(value, start, start + size, axis=4)
+
+        piece = (bands, 2, size, width)
+        raw_g = lax.ppermute(cut(g_own), "energy", RAW).reshape(piece)
+        raw_l = lax.ppermute(cut(l_mate), "energy", RAW_ONE).reshape(piece)
+        rows = rows_of(g_own.shape, start, size)
+        partial = pl.pallas_call(
+            partial_kernel,
+            out_shape=jax.ShapeDtypeStruct(piece, bf16),
+            in_specs=[scalars()] + [rows] * 4 + [whole(piece)],
+            out_specs=whole(piece),
+            compiler_params=params(),
+            grid=(1,),
+        name="partial",
+        )(place, l_own, g_own, l_mate, g_mate, raw_l)
+        arrived = lax.ppermute(partial, "energy", PARTIAL)
+        raw_g_mate = lax.ppermute(raw_g, "energy", ON_CHIP)
+        term = (2, 2, size, width)
+        near, far, own = pl.pallas_call(
+            lambda *refs: polar_kernel(1.0 / math.sqrt(energies), *refs),
+            out_shape=(jax.ShapeDtypeStruct(term, bf16),) * 3,
+            in_specs=[scalars()]
+            + [rows] * 4
+            + [whole(piece)] * 4
+            + [whole(r.shape) for r in right],
+            out_specs=(whole(term),) * 3,
+            scratch_shapes=[pltpu.VMEM((bands, 2 * size, 2 * width), bf16)],
+            compiler_params=params(),
+            grid=(1,),
+        name="polar",
+        )(place, l_own, g_own, l_mate, g_mate, raw_g, raw_g_mate, raw_l, arrived, *rights)
+        nears.append(lax.ppermute(near, "slab", near_pairs))
+        fars.append(lax.ppermute(far, "slab", far_pairs))
+        owns.append(own)
+
+    count = len(owns)
+    anywhere = pl.BlockSpec(memory_space=pl.ANY)
+    w_diag, w_upper = pl.pallas_call(
+        lambda *refs: final_kernel(count, *refs),
+        out_shape=(jax.ShapeDtypeStruct(square, bf16),) * 2,
+        in_specs=[anywhere] * (3 * count) + [whole((2 * width, 6 * width))],
+        out_specs=(whole(square),) * 2,
+        scratch_shapes=[
+            pltpu.VMEM((3, 2, 2, width, width), bf16),
+            pltpu.SemaphoreType.DMA((3, count)),
+        ],
+        compiler_params=params(),
+        grid=(1,),
+        name="final",
+    )(*owns, *nears, *fars, left)
+    shape = (1, 1) + square
+    return w_diag.reshape(shape), w_upper.reshape(shape)
+
+
+def per_device(g_lesser, g_greater, v_diag, v_upper):
+    paired = lax.axis_size("energy") == 4 and lax.axis_size("slab") % 2 == 0
+    if paired and g_lesser.shape[0] == 1 and v_diag.shape[0] == 1:
+        return exchanged(g_lesser, g_greater, v_diag, v_upper)
+    return general(g_lesser, g_greater, v_diag, v_upper)
+
+
 def solution(mesh):
     placed = (
         P("energy", "slab", None, None, None, None),

time: 120 us -> 73.4 us (0.61)
  waiting for transfers between devices: 58.3 us -> 17.7 us
  matrix products: 22.5 us -> 0 us
  Pallas kernels: 0 us -> 13.5 us
  starting transfers between devices: 27 us -> 34.3 us
  local copies, waits for them, and re-layouts: 7.24 us -> 4.35 us
    all_to_all x3 -> x0, waiting for transfers between devices: 23.5 us -> none  [the longest x1 11.1 us: per_device(): lax.all_to_all(g_greater, 'energy', split_axis=4, concat_axis=0, tiled=True)]
    dot_general x68 -> x0, matrix products: 22.5 us -> none  [the longest x12 11.5 us: transform(): jnp.einsum('fn,n...->f...', table, signal, precision=lax.Precision.HIGH)]
    ppermute x4 -> x24, starting transfers between devices: 12.8 us -> 34.3 us  [the longest x3 10.5 us: exchanged(): fars.append(lax.ppermute(far, 'slab', far_pairs))]
    ppermute x4 -> x24, waiting for transfers between devices: 34.8 us -> 17.7 us  [the longest x3 7.49 us: exchanged(): nears.append(lax.ppermute(near, 'slab', near_pairs))]
    all_to_all x3 -> x0, starting transfers between devices: 14.2 us -> none  [the longest x1 5.12 us: per_device(): lax.all_to_all(g_lesser, 'energy', split_axis=4, concat_axis=0, tiled=True)]
    pallas_call x0 -> x8, Pallas kernels: none -> 13.5 us  [the longest x3 7.04 us: exchanged(): pl.pallas_call(lambda *refs: polar_kernel(1.0 / math.sqrt(energies), *ref...]
    unnamed x10 -> x18, local copies, waits for them, and re-layouts: 4.55 us -> 0.92 us
    slice x0 -> x4, local copies, waits for them, and re-layouts: none -> 3.42 us  [cut(): return lax.slice_in_dim(value, start, start + size, axis=4)]
  transfers between devices with their start and end apart: 7 -> 24, of which waited for: 5 -> 5; matrix products, arithmetic and copies ran while one was open for 10% -> 7% of each run, Pallas kernels for 0% -> 15%
where the time goes in v1:
time: 73.4 us; the launch traced here: 72.8 us
  starting transfers between devices  34.3 us (47%)
  waiting for transfers between devices  17.7 us (24%)
  Pallas kernels  13.5 us (18%)
  local copies, waits for them, and re-layouts  4.35 us (6%)
  other arithmetic  1.92 us (3%)
  between operations  1.01 us (1%)
    ppermute x3, starting transfers between devices, exchanged(): fars.append(lax.ppermute(far, 'slab', far_pairs))  10.5 us
    ppermute x3, starting transfers between devices, exchanged(): raw_g = lax.ppermute(cut(g_own), 'energy', RAW).reshape(piece)  9.52 us
    ppermute x3, waiting for transfers between devices, exchanged(): nears.append(lax.ppermute(near, 'slab', near_pairs))  7.49 us
    pallas_call x3, Pallas kernels, exchanged(): pl.pallas_call(lambda *refs: polar_kernel(1.0 / math.sqrt(energies), *ref...  7.04 us
    ppermute x3, waiting for transfers between devices, exchanged(): arrived = lax.ppermute(partial, 'energy', PARTIAL)  5.86 us
    ppermute x3, waiting for transfers between devices, exchanged(): raw_g = lax.ppermute(cut(g_own), 'energy', RAW).reshape(piece)  4.32 us
    ppermute x3, starting transfers between devices, exchanged(): arrived = lax.ppermute(partial, 'energy', PARTIAL)  3.85 us
    slice x4, local copies, waits for them, and re-layouts, cut(): return lax.slice_in_dim(value, start, start + size, axis=4)  3.42 us
  transfers between devices with their start and end apart: 24, of which 5 were waited for; matrix products, arithmetic and copies ran while one was open for 7% of the time, Pallas kernels for 15%

profile of v1, /device:TPU:26, one launch (start us, length us, event | category | flops | bytes accessed | tf_op | source)
XLA Modules:
  0.0 72.8 jit_solution(16259448150585260607)
XLA Ops:
  0.6 0.1 collective-permute-start
  0.7 0.5 collective-permute-start.1
  1.2 1.9 %fusion.1 = (bf16[1,1,3,2,80,256]{5,4,3,2,1,0:T(8,128)(2,1)}, bf16[1,1,3,2,80,256]{5,4,3,2,1,0:T(8,128)(2,1)}) fusion(bf16[1,1,3,2,256,256]{5,4,3,2,1,0:T(8,128)(2,1)} %refs_2_.5), kind=kLoop, calls=%fused_computation.4 | loop fusion | bytes 983040 | tf_op jit(solution)/shard_map/slice | solution.py:417
  3.1 3.1 %collective-permute-start.10 = (bf16[1,1,3,2,80,256]{5,4,3,2,1,0:T(8,128)(2,1)}, bf16[1,1,3,2,80,256]{5,4,3,2,1,0:T(8,128)(2,1)}, u32[]{:S(2)}, u32[]{:S(2)}) collective-permute-start(bf16[1,1,3,2,80,256]{5,4,3,2,1,0:T(8,128)(2,1)} %get-tuple-element.39), channel_id=1, source_target_pairs={{16,0},{24,8},{17,1},{25,9},{18,2},{26,10},{19,3},{27,11},{20,4},{... | collective-permute-start | bytes 737288 | tf_op jit(solution)/shard_map/ppermute | solution.py:420
  6.2 1.3 %collective-permute-start.14 = (bf16[1,1,3,2,80,256]{5,4,3,2,1,0:T(8,128)(2,1)}, bf16[1,1,3,2,80,256]{5,4,3,2,1,0:T(8,128)(2,1)S(1)}, u32[]{:S(2)}, u32[]{:S(2)}) collective-permute-start(bf16[1,1,3,2,80,256]{5,4,3,2,1,0:T(8,128)(2,1)} %get-tuple-element.38), channel_id=1, source_target_pairs={{16,0},{24,8},{17,1},{25,9},{18,2},{26,10},{19,3},{27,11},{20,4},{... | collective-permute-start | bytes 737288 | tf_op jit(solution)/shard_map/ppermute | solution.py:420
  7.5 0.0 copy-start.1
  7.5 1.8 %broadcast_select_fusion = (bf16[2,256,256]{2,1,0:T(8,128)(2,1)S(1)}, bf16[2,256,256]{2,1,0:T(8,128)(2,1)}) fusion(pred[]{:T(512)S(6)} %eq.10, bf16[1,2,256,256]{3,2,1,0:T(8,128)(2,1)} %param.6, bf16[1,2,256,256]{3,2,1,0:T(8,128)(2,1)} %param.7, pred[]{:T(512)S(6)} %eq.9), kind=kLoop, calls=%fused_computation.1 | loop fusion | flops 262144 | bytes 1048578 | tf_op jit(solution)/shard_map/jit(_where)/select_n | solution.py:395
  9.4 1.4 %collective-permute-start.6 = (bf16[2,256,256]{2,1,0:T(8,128)(2,1)S(1)}, bf16[2,256,256]{2,1,0:T(8,128)(2,1)}, u32[]{:S(2)}, u32[]{:S(2)}) collective-permute-start(bf16[2,256,256]{2,1,0:T(8,128)(2,1)S(1)} %get-tuple-element.34), channel_id=1, source_target_pairs={{0,1},{1,0},{2,3},{3,2},{4,5},{5,4},{6,7},{7,6},{8,9},{9,8},{10,11... | collective-permute-start | bytes 786440 | tf_op jit(solution)/shard_map/ppermute | solution.py:396
  10.9 1.3 %collective-permute-done.10 = bf16[1,1,3,2,80,256]{5,4,3,2,1,0:T(8,128)(2,1)} collective-permute-done((bf16[1,1,3,2,80,256]{5,4,3,2,1,0:T(8,128)(2,1)}, bf16[1,1,3,2,80,256]{5,4,3,2,1,0:T(8,128)(2,1)}, u32[]{:S(2)}, u32[]{:S(2)}) %collective-permute-start.10) | collective-permute-done | bytes 245792 | tf_op jit(solution)/shard_map/ppermute | solution.py:420
  12.2 3.3 %collective-permute-start.8 = (bf16[2,256,256]{2,1,0:T(8,128)(2,1)S(1)}, bf16[2,256,256]{2,1,0:T(8,128)(2,1)}, u32[]{:S(2)}, u32[]{:S(2)}) collective-permute-start(bf16[2,256,256]{2,1,0:T(8,128)(2,1)S(1)} %get-tuple-element.34), channel_id=1, source_target_pairs={{1,2},{3,4},{5,6},{2,1},{4,3},{6,5},{9,10},{11,12},{13,14},{10,9},... | collective-permute-start | bytes 786440 | tf_op jit(solution)/shard_map/ppermute | solution.py:397
  15.5 5.1 %collective-permute-start.2 = (bf16[1,1,3,2,96,256]{5,4,3,2,1,0:T(8,128)(2,1)S(1)}, bf16[1,1,3,2,96,256]{5,4,3,2,1,0:T(8,128)(2,1)}, u32[]{:S(2)}, u32[]{:S(2)}) collective-permute-start(bf16[1,1,3,2,96,256]{5,4,3,2,1,0:T(8,128)(2,1)S(1)} %slice.18), channel_id=1, source_target_pairs={{16,0},{24,8},{17,1},{25,9},{18,2},{26,10},{19,3},{27,11},{20,4},{... | collective-permute-start | bytes 884744 | tf_op jit(solution)/shard_map/ppermute | solution.py:420
  20.6 0.8 %fusion = (bf16[1,1,3,2,80,256]{5,4,3,2,1,0:T(8,128)(2,1)}, bf16[1,1,3,2,80,256]{5,4,3,2,1,0:T(8,128)(2,1)}) fusion(bf16[1,1,3,2,256,256]{5,4,3,2,1,0:T(8,128)(2,1)S(1)} %collective-permute-done.l_mate.refs_3_), kind=kLoop, calls=%fused_computation.3 | loop fusion | bytes 983040 | tf_op jit(solution)/shard_map/slice | solution.py:417
  21.4 1.4 %collective-permute-start.12 = (bf16[1,1,3,2,80,256]{5,4,3,2,1,0:T(8,128)(2,1)}, bf16[1,1,3,2,80,256]{5,4,3,2,1,0:T(8,128)(2,1)}, u32[]{:S(2)}, u32[]{:S(2)}) collective-permute-start(bf16[1,1,3,2,80,256]{5,4,3,2,1,0:T(8,128)(2,1)} %get-tuple-element.37), channel_id=1, source_target_pairs={{24,8},{25,9},{26,10},{27,11},{28,12},{29,13},{30,14},{31,15}} | collective-permute-start | bytes 737288 | tf_op jit(solution)/shard_map/ppermute | solution.py:421
  22.8 0.7 slice.24
  23.5 0.7 collective-permute-start.4
  24.2 0.1 collective-permute-start.11
  24.3 3.0 %collective-permute-done.2 = bf16[1,1,3,2,96,256]{5,4,3,2,1,0:T(8,128)(2,1)} collective-permute-done((bf16[1,1,3,2,96,256]{5,4,3,2,1,0:T(8,128)(2,1)S(1)}, bf16[1,1,3,2,96,256]{5,4,3,2,1,0:T(8,128)(2,1)}, u32[]{:S(2)}, u32[]{:S(2)}) %collective-permute-start.2) | collective-permute-done | bytes 294944 | tf_op jit(solution)/shard_map/ppermute | solution.py:420
  27.3 1.3 %collective-permute-start.16 = (bf16[1,1,3,2,80,256]{5,4,3,2,1,0:T(8,128)(2,1)}, bf16[1,1,3,2,80,256]{5,4,3,2,1,0:T(8,128)(2,1)}, u32[]{:S(2)}, u32[]{:S(2)}) collective-permute-start(bf16[1,1,3,2,80,256]{5,4,3,2,1,0:T(8,128)(2,1)} %get-tuple-element.36), channel_id=1, source_target_pairs={{24,8},{25,9},{26,10},{27,11},{28,12},{29,13},{30,14},{31,15}} | collective-permute-start | bytes 737288 | tf_op jit(solution)/shard_map/ppermute | solution.py:421
  28.6 0.5 collective-permute-start.9
  29.1 0.1 pad_add_fusion.place.refs_0_
  29.2 1.0 %partial.4 = bf16[3,2,80,256]{3,2,1,0:T(8,128)(2,1)S(1)} custom-call(s32[3]{0:T(128)S(1)} %pad_add_fusion.place.refs_0_, bf16[1,1,3,2,256,256]{5,4,3,2,1,0:T(8,128)(2,1)S(1)} %copy-done.1, bf16[1,1,3,2,256,256]{5,4,3,2,1,0:T(8,128)(2,1)S(1)} %copy-done, bf16[1,1,3,2,256,256]{5,4,3,2,1,0:T(8,128)(2,1)S(1)} %collective-permute-done.l_mate.refs_3_, ...), custom_call_target="tpu_custom_call" | custom-call | tf_op jit(solution)/shard_map/partial/pallas_call | solution.py:423
  30.3 1.3 %collective-permute-start.13 = (bf16[3,2,80,256]{3,2,1,0:T(8,128)(2,1)S(1)}, bf16[3,2,80,256]{3,2,1,0:T(8,128)(2,1)S(1)}, u32[]{:S(2)}, u32[]{:S(2)}) collective-permute-start(bf16[3,2,80,256]{3,2,1,0:T(8,128)(2,1)S(1)} %partial.4), channel_id=1, source_target_pairs={{0,16},{8,24},{1,17},{9,25},{2,18},{10,26},{3,19},{11,27},{4,20},{... | collective-permute-start | bytes 737288 | tf_op jit(solution)/shard_map/ppermute | solution.py:432
  31.6 0.6 partial.3
  32.1 0.2 collective-permute-start.3
  32.3 1.3 %collective-permute-start.5 = (bf16[3,2,96,256]{3,2,1,0:T(8,128)(2,1)S(1)}, bf16[3,2,96,256]{3,2,1,0:T(8,128)(2,1)S(1)}, u32[]{:S(2)}, u32[]{:S(2)}) collective-permute-start(bf16[3,2,96,256]{3,2,1,0:T(8,128)(2,1)S(1)} %partial.3), channel_id=1, source_target_pairs={{0,16},{8,24},{1,17},{9,25},{2,18},{10,26},{3,19},{11,27},{4,20},{... | collective-permute-start | bytes 884744 | tf_op jit(solution)/shard_map/ppermute | solution.py:432
  33.6 0.0 copy-start.8
  33.6 0.0 copy-start.5
  33.6 0.0 copy-start.6
  33.6 1.1 %partial.5 = bf16[3,2,80,256]{3,2,1,0:T(8,128)(2,1)S(1)} custom-call(s32[3]{0:T(128)S(1)} %pad_add_fusion.place.refs_0_, bf16[1,1,3,2,256,256]{5,4,3,2,1,0:T(8,128)(2,1)S(1)} %copy-done.1, bf16[1,1,3,2,256,256]{5,4,3,2,1,0:T(8,128)(2,1)S(1)} %copy-done, bf16[1,1,3,2,256,256]{5,4,3,2,1,0:T(8,128)(2,1)S(1)} %collective-permute-done.l_mate.refs_3_, ...), custom_call_target="tpu_custom_call" | custom-call | tf_op jit(solution)/shard_map/partial/pallas_call | solution.py:423
  34.8 0.8 %collective-permute-start.15 = (bf16[3,2,80,256]{3,2,1,0:T(8,128)(2,1)S(1)}, bf16[3,2,80,256]{3,2,1,0:T(8,128)(2,1)S(1)}, u32[]{:S(2)}, u32[]{:S(2)}) collective-permute-start(bf16[3,2,80,256]{3,2,1,0:T(8,128)(2,1)S(1)} %bitcast.19), channel_id=1, source_target_pairs={{0,8},{8,0},{16,24},{24,16},{1,9},{9,1},{17,25},{25,17},{2,10},{10... | collective-permute-start | bytes 737288 | tf_op jit(solution)/shard_map/ppermute | solution.py:433
  35.5 0.0 collective-permute-done.9.far_mate
  35.5 1.3 %collective-permute-start.17 = (bf16[3,2,80,256]{3,2,1,0:T(8,128)(2,1)S(1)}, bf16[3,2,80,256]{3,2,1,0:T(8,128)(2,1)S(1)}, u32[]{:S(2)}, u32[]{:S(2)}) collective-permute-start(bf16[3,2,80,256]{3,2,1,0:T(8,128)(2,1)S(1)} %partial.5), channel_id=1, source_target_pairs={{0,16},{8,24},{1,17},{9,25},{2,18},{10,26},{3,19},{11,27},{4,20},{... | collective-permute-start | bytes 737288 | tf_op jit(solution)/shard_map/ppermute | solution.py:432
  36.9 1.4 %coupling.1 = (bf16[1024,256]{1,0:T(8,128)(2,1)S(1)}, bf16[1536,256]{1,0:T(8,128)(2,1)S(1)}, bf16[1024,256]{1,0:T(8,128)(2,1)S(1)}, bf16[512,256]{1,0:T(8,128)(2,1)S(1)}, bf16[512,1536]{1,0:T(8,128)(2,1)S(1)}) custom-call(s32[3]{0:T(128)S(1)} %pad_add_fusion.place.refs_0_, bf16[2,256,256]{2,1,0:T(8,128)(2,1)S(1)} %bitcast.18, ...), custom_call_target="tpu_custom_call" | custom-call | tf_op jit(solution)/shard_map/coupling/pallas_call | solution.py:404
  38.2 0.9 %copy-done.4 = bf16[1536,256]{1,0:T(8,128)(2,1)} copy-done((bf16[1536,256]{1,0:T(8,128)(2,1)}, bf16[1536,256]{1,0:T(8,128)(2,1)S(1)}, u32[]{:S(2)}) %copy-start.4) | copy-done | bytes 786456
  39.1 2.1 %collective-permute-done.13.refs_8_ = bf16[3,2,80,256]{3,2,1,0:T(8,128)(2,1)S(1)} collective-permute-done((bf16[3,2,80,256]{3,2,1,0:T(8,128)(2,1)S(1)}, bf16[3,2,80,256]{3,2,1,0:T(8,128)(2,1)S(1)}, u32[]{:S(2)}, u32[]{:S(2)}) %collective-permute-start.13) | collective-permute-done | bytes 245792 | tf_op jit(solution)/shard_map/ppermute | solution.py:432
  41.2 2.4 %polar.4 = (bf16[2,2,80,256]{3,2,1,0:T(8,128)(2,1)S(1)}, bf16[2,2,80,256]{3,2,1,0:T(8,128)(2,1)S(1)}, bf16[2,2,80,256]{3,2,1,0:T(8,128)(2,1)S(1)}) custom-call(s32[3]{0:T(128)S(1)} %pad_add_fusion.place.refs_0_, bf16[1,1,3,2,256,256]{5,4,3,2,1,0:T(8,128)(2,1)S(1)} %copy-done.1, bf16[1,1,3,2,256,256]{5,4,3,2,1,0:T(8,128)(2,1)S(1)} %copy-done, ...), custom_call_target="tpu_custom_call" | custom-call | tf_op jit(solution)/shard_map/polar/pallas_call | solution.py:435
  43.6 0.1 collective-permute-start.19
  43.7 3.8 %collective-permute-done.5.refs_8_ = bf16[3,2,96,256]{3,2,1,0:T(8,128)(2,1)S(1)} collective-permute-done((bf16[3,2,96,256]{3,2,1,0:T(8,128)(2,1)S(1)}, bf16[3,2,96,256]{3,2,1,0:T(8,128)(2,1)S(1)}, u32[]{:S(2)}, u32[]{:S(2)}) %collective-permute-start.5) | collective-permute-done | bytes 294944 | tf_op jit(solution)/shard_map/ppermute | solution.py:432
  47.5 2.4 %polar.3 = (bf16[2,2,96,256]{3,2,1,0:T(8,128)(2,1)S(1)}, bf16[2,2,96,256]{3,2,1,0:T(8,128)(2,1)S(1)}, bf16[2,2,96,256]{3,2,1,0:T(8,128)(2,1)S(1)}) custom-call(s32[3]{0:T(128)S(1)} %pad_add_fusion.place.refs_0_, bf16[1,1,3,2,256,256]{5,4,3,2,1,0:T(8,128)(2,1)S(1)} %copy-done.1, bf16[1,1,3,2,256,256]{5,4,3,2,1,0:T(8,128)(2,1)S(1)} %copy-done, ...), custom_call_target="tpu_custom_call" | custom-call | tf_op jit(solution)/shard_map/polar/pallas_call | solution.py:435
  49.9 0.1 collective-permute-start.18
  50.0 3.8 %collective-permute-start.21 = (bf16[2,2,96,256]{3,2,1,0:T(8,128)(2,1)S(1)}, bf16[2,2,96,256]{3,2,1,0:T(8,128)(2,1)S(1)}, u32[]{:S(2)}, u32[]{:S(2)}) collective-permute-start(bf16[2,2,96,256]{3,2,1,0:T(8,128)(2,1)S(1)} %get-tuple-element.28), channel_id=1, source_target_pairs={{1,2},{3,4},{5,6},{2,1},{4,3},{6,5},{9,10},{11,12},{13,14},{10,9},... | collective-permute-start | bytes 589832 | tf_op jit(solution)/shard_map/ppermute | solution.py:449
  53.8 0.0 collective-permute-done.15.refs_6_
  53.8 2.2 %polar.5 = (bf16[2,2,80,256]{3,2,1,0:T(8,128)(2,1)S(1)}, bf16[2,2,80,256]{3,2,1,0:T(8,128)(2,1)S(1)}, bf16[2,2,80,256]{3,2,1,0:T(8,128)(2,1)S(1)}) custom-call(s32[3]{0:T(128)S(1)} %pad_add_fusion.place.refs_0_, bf16[1,1,3,2,256,256]{5,4,3,2,1,0:T(8,128)(2,1)S(1)} %copy-done.1, bf16[1,1,3,2,256,256]{5,4,3,2,1,0:T(8,128)(2,1)S(1)} %copy-done, ...), custom_call_target="tpu_custom_call" | custom-call | tf_op jit(solution)/shard_map/polar/pallas_call | solution.py:435
  56.1 0.1 collective-permute-start.20
  56.1 3.8 %collective-permute-start.22 = (bf16[2,2,80,256]{3,2,1,0:T(8,128)(2,1)S(1)}, bf16[2,2,80,256]{3,2,1,0:T(8,128)(2,1)S(1)}, u32[]{:S(2)}, u32[]{:S(2)}) collective-permute-start(bf16[2,2,80,256]{3,2,1,0:T(8,128)(2,1)S(1)} %get-tuple-element.29), channel_id=1, source_target_pairs={{1,2},{3,4},{5,6},{2,1},{4,3},{6,5},{9,10},{11,12},{13,14},{10,9},... | collective-permute-start | bytes 491528 | tf_op jit(solution)/shard_map/ppermute | solution.py:449
  60.0 2.9 %collective-permute-start.23 = (bf16[2,2,80,256]{3,2,1,0:T(8,128)(2,1)S(1)}, bf16[2,2,80,256]{3,2,1,0:T(8,128)(2,1)S(1)}, u32[]{:S(2)}, u32[]{:S(2)}) collective-permute-start(bf16[2,2,80,256]{3,2,1,0:T(8,128)(2,1)S(1)} %get-tuple-element.30), channel_id=1, source_target_pairs={{1,2},{3,4},{5,6},{2,1},{4,3},{6,5},{9,10},{11,12},{13,14},{10,9},... | collective-permute-start | bytes 491528 | tf_op jit(solution)/shard_map/ppermute | solution.py:449
  62.9 7.5 %collective-permute-done.20.refs_5_ = bf16[2,2,80,256]{3,2,1,0:T(8,128)(2,1)S(1)} collective-permute-done((bf16[2,2,80,256]{3,2,1,0:T(8,128)(2,1)S(1)}, bf16[2,2,80,256]{3,2,1,0:T(8,128)(2,1)S(1)}, u32[]{:S(2)}, u32[]{:S(2)}) %collective-permute-start.20) | collective-permute-done | bytes 163872 | tf_op jit(solution)/shard_map/ppermute | solution.py:448
  70.4 2.4 %final.1 = (bf16[2,256,256]{2,1,0:T(8,128)(2,1)}, bf16[2,256,256]{2,1,0:T(8,128)(2,1)}) custom-call(bf16[2,2,96,256]{3,2,1,0:T(8,128)(2,1)S(1)} %get-tuple-element.22.refs_0_, bf16[2,2,80,256]{3,2,1,0:T(8,128)(2,1)S(1)} %get-tuple-element.23.refs_1_, bf16[2,2,80,256]{3,2,1,0:T(8,128)(2,1)S(1)} %get-tuple-element.24.refs_2_, ...), custom_call_target="tpu_custom_call" | custom-call | tf_op jit(solution)/shard_map/final/pallas_call | solution.py:454
  (32 shorter events, 0.1 us)
Async XLA Ops:
  0.6 10.2 %copy-start = (bf16[1,1,3,2,256,256]{5,4,3,2,1,0:T(8,128)(2,1)S(1)}, bf16[1,1,3,2,256,256]{5,4,3,2,1,0:T(8,128)(2,1)}, u32[]{:S(2)}) copy-start(bf16[1,1,3,2,256,256]{5,4,3,2,1,0:T(8,128)(2,1)} %refs_2_.5) | copy-start | bytes 2359300
  0.6 14.8 %collective-permute-start = (bf16[1,1,3,2,256,256]{5,4,3,2,1,0:T(8,128)(2,1)}, bf16[1,1,3,2,256,256]{5,4,3,2,1,0:T(8,128)(2,1)S(1)}, u32[]{:S(2)}, u32[]{:S(2)}) collective-permute-start(bf16[1,1,3,2,256,256]{5,4,3,2,1,0:T(8,128)(2,1)} %refs_1_.5), channel_id=1, source_target_pairs={{0,8},{8,0},{16,24},{24,16},{1,9},{9,1},{17,25},{25,17},{2,10},{10... | collective-permute-start | bytes 2359304 | tf_op jit(solution)/shard_map/ppermute | solution.py:390
  0.7 27.9 %collective-permute-start.1 = (bf16[1,1,3,2,256,256]{5,4,3,2,1,0:T(8,128)(2,1)}, bf16[1,1,3,2,256,256]{5,4,3,2,1,0:T(8,128)(2,1)S(1)}, u32[]{:S(2)}, u32[]{:S(2)}) collective-permute-start(bf16[1,1,3,2,256,256]{5,4,3,2,1,0:T(8,128)(2,1)} %refs_2_.5), channel_id=1, source_target_pairs={{0,8},{8,0},{16,24},{24,16},{1,9},{9,1},{17,25},{25,17},{2,10},{10... | collective-permute-start | bytes 2359304 | tf_op jit(solution)/shard_map/ppermute | solution.py:391
  3.1 9.1 %collective-permute-start.10 = (bf16[1,1,3,2,80,256]{5,4,3,2,1,0:T(8,128)(2,1)}, bf16[1,1,3,2,80,256]{5,4,3,2,1,0:T(8,128)(2,1)}, u32[]{:S(2)}, u32[]{:S(2)}) collective-permute-start(bf16[1,1,3,2,80,256]{5,4,3,2,1,0:T(8,128)(2,1)} %get-tuple-element.39), channel_id=1, source_target_pairs={{16,0},{24,8},{17,1},{25,9},{18,2},{26,10},{19,3},{27,11},{20,4},{... | collective-permute-start | bytes 737288 | tf_op jit(solution)/shard_map/ppermute | solution.py:420
  6.2 15.2 %collective-permute-start.14 = (bf16[1,1,3,2,80,256]{5,4,3,2,1,0:T(8,128)(2,1)}, bf16[1,1,3,2,80,256]{5,4,3,2,1,0:T(8,128)(2,1)S(1)}, u32[]{:S(2)}, u32[]{:S(2)}) collective-permute-start(bf16[1,1,3,2,80,256]{5,4,3,2,1,0:T(8,128)(2,1)} %get-tuple-element.38), channel_id=1, source_target_pairs={{16,0},{24,8},{17,1},{25,9},{18,2},{26,10},{19,3},{27,11},{20,4},{... | collective-permute-start | bytes 737288 | tf_op jit(solution)/shard_map/ppermute | solution.py:420
  7.5 21.7 %copy-start.1 = (bf16[1,1,3,2,256,256]{5,4,3,2,1,0:T(8,128)(2,1)S(1)}, bf16[1,1,3,2,256,256]{5,4,3,2,1,0:T(8,128)(2,1)}, u32[]{:S(2)}) copy-start(bf16[1,1,3,2,256,256]{5,4,3,2,1,0:T(8,128)(2,1)} %refs_1_.5) | copy-start | bytes 2359300
  9.4 14.1 %collective-permute-start.6 = (bf16[2,256,256]{2,1,0:T(8,128)(2,1)S(1)}, bf16[2,256,256]{2,1,0:T(8,128)(2,1)}, u32[]{:S(2)}, u32[]{:S(2)}) collective-permute-start(bf16[2,256,256]{2,1,0:T(8,128)(2,1)S(1)} %get-tuple-element.34), channel_id=1, source_target_pairs={{0,1},{1,0},{2,3},{3,2},{4,5},{5,4},{6,7},{7,6},{8,9},{9,8},{10,11... | collective-permute-start | bytes 786440 | tf_op jit(solution)/shard_map/ppermute | solution.py:396
  12.2 12.0 %collective-permute-start.8 = (bf16[2,256,256]{2,1,0:T(8,128)(2,1)S(1)}, bf16[2,256,256]{2,1,0:T(8,128)(2,1)}, u32[]{:S(2)}, u32[]{:S(2)}) collective-permute-start(bf16[2,256,256]{2,1,0:T(8,128)(2,1)S(1)} %get-tuple-element.34), channel_id=1, source_target_pairs={{1,2},{3,4},{5,6},{2,1},{4,3},{6,5},{9,10},{11,12},{13,14},{10,9},... | collective-permute-start | bytes 786440 | tf_op jit(solution)/shard_map/ppermute | solution.py:397
  15.5 11.8 %collective-permute-start.2 = (bf16[1,1,3,2,96,256]{5,4,3,2,1,0:T(8,128)(2,1)S(1)}, bf16[1,1,3,2,96,256]{5,4,3,2,1,0:T(8,128)(2,1)}, u32[]{:S(2)}, u32[]{:S(2)}) collective-permute-start(bf16[1,1,3,2,96,256]{5,4,3,2,1,0:T(8,128)(2,1)S(1)} %slice.18), channel_id=1, source_target_pairs={{16,0},{24,8},{17,1},{25,9},{18,2},{26,10},{19,3},{27,11},{20,4},{... | collective-permute-start | bytes 884744 | tf_op jit(solution)/shard_map/ppermute | solution.py:420
  21.4 2.1 %copy-start.7 = (bf16[1,1,3,2,80,256]{5,4,3,2,1,0:T(8,128)(2,1)}, bf16[1,1,3,2,80,256]{5,4,3,2,1,0:T(8,128)(2,1)S(1)}, u32[]{:S(2)}) copy-start(bf16[1,1,3,2,80,256]{5,4,3,2,1,0:T(8,128)(2,1)S(1)} %collective-permute-done.14) | copy-start | bytes 737284
  21.4 7.2 %collective-permute-start.12 = (bf16[1,1,3,2,80,256]{5,4,3,2,1,0:T(8,128)(2,1)}, bf16[1,1,3,2,80,256]{5,4,3,2,1,0:T(8,128)(2,1)}, u32[]{:S(2)}, u32[]{:S(2)}) collective-permute-start(bf16[1,1,3,2,80,256]{5,4,3,2,1,0:T(8,128)(2,1)} %get-tuple-element.37), channel_id=1, source_target_pairs={{24,8},{25,9},{26,10},{27,11},{28,12},{29,13},{30,14},{31,15}} | collective-permute-start | bytes 737288 | tf_op jit(solution)/shard_map/ppermute | solution.py:421
  23.5 6.8 %collective-permute-start.4 = (bf16[1,1,3,2,96,256]{5,4,3,2,1,0:T(8,128)(2,1)}, bf16[1,1,3,2,96,256]{5,4,3,2,1,0:T(8,128)(2,1)S(1)}, u32[]{:S(2)}, u32[]{:S(2)}) collective-permute-start(bf16[1,1,3,2,96,256]{5,4,3,2,1,0:T(8,128)(2,1)} %slice.24), channel_id=1, source_target_pairs={{24,8},{25,9},{26,10},{27,11},{28,12},{29,13},{30,14},{31,15}} | collective-permute-start | bytes 884744 | tf_op jit(solution)/shard_map/ppermute | solution.py:421
  24.2 8.0 %collective-permute-start.11 = (bf16[3,2,80,256]{3,2,1,0:T(8,128)(2,1)}, bf16[3,2,80,256]{3,2,1,0:T(8,128)(2,1)}, u32[]{:S(2)}, u32[]{:S(2)}) collective-permute-start(bf16[3,2,80,256]{3,2,1,0:T(8,128)(2,1)} %bitcast.7.refs_5_), channel_id=1, source_target_pairs={{0,8},{8,0},{16,24},{24,16},{1,9},{9,1},{17,25},{25,17},{2,10},{10... | collective-permute-start | bytes 737288 | tf_op jit(solution)/shard_map/ppermute | solution.py:433
  27.3 5.0 %collective-permute-start.16 = (bf16[1,1,3,2,80,256]{5,4,3,2,1,0:T(8,128)(2,1)}, bf16[1,1,3,2,80,256]{5,4,3,2,1,0:T(8,128)(2,1)}, u32[]{:S(2)}, u32[]{:S(2)}) collective-permute-start(bf16[1,1,3,2,80,256]{5,4,3,2,1,0:T(8,128)(2,1)} %get-tuple-element.36), channel_id=1, source_target_pairs={{24,8},{25,9},{26,10},{27,11},{28,12},{29,13},{30,14},{31,15}} | collective-permute-start | bytes 737288 | tf_op jit(solution)/shard_map/ppermute | solution.py:421
  28.6 12.6 %copy-start.2 = (bf16[1,1,3,2,256,256]{5,4,3,2,1,0:T(8,128)(2,1)}, bf16[1,1,3,2,256,256]{5,4,3,2,1,0:T(8,128)(2,1)S(1)}, u32[]{:S(2)}) copy-start(bf16[1,1,3,2,256,256]{5,4,3,2,1,0:T(8,128)(2,1)S(1)} %collective-permute-done.1.g_mate.refs_4_) | copy-start | bytes 2359300
  28.6 6.1 %collective-permute-start.7 = (bf16[2,256,256]{2,1,0:T(8,128)(2,1)}, bf16[2,256,256]{2,1,0:T(8,128)(2,1)S(1)}, u32[]{:S(2)}, u32[]{:S(2)}) collective-permute-start(bf16[2,256,256]{2,1,0:T(8,128)(2,1)} %collective-permute-done.6.near), channel_id=1, source_target_pairs={{0,8},{8,0},{16,24},{24,16},{1,9},{9,1},{17,25},{25,17},{2,10},{10... | collective-permute-start | bytes 786440 | tf_op jit(solution)/shard_map/ppermute | solution.py:398
  28.6 6.9 %collective-permute-start.9 = (bf16[2,256,256]{2,1,0:T(8,128)(2,1)}, bf16[2,256,256]{2,1,0:T(8,128)(2,1)S(1)}, u32[]{:S(2)}, u32[]{:S(2)}) collective-permute-start(bf16[2,256,256]{2,1,0:T(8,128)(2,1)} %collective-permute-done.8.far), channel_id=1, source_target_pairs={{0,8},{8,0},{16,24},{24,16},{1,9},{9,1},{17,25},{25,17},{2,10},{10... | collective-permute-start | bytes 786440 | tf_op jit(solution)/shard_map/ppermute | solution.py:399
  30.3 10.9 %collective-permute-start.13 = (bf16[3,2,80,256]{3,2,1,0:T(8,128)(2,1)S(1)}, bf16[3,2,80,256]{3,2,1,0:T(8,128)(2,1)S(1)}, u32[]{:S(2)}, u32[]{:S(2)}) collective-permute-start(bf16[3,2,80,256]{3,2,1,0:T(8,128)(2,1)S(1)} %partial.4), channel_id=1, source_target_pairs={{0,16},{8,24},{1,17},{9,25},{2,18},{10,26},{3,19},{11,27},{4,20},{... | collective-permute-start | bytes 737288 | tf_op jit(solution)/shard_map/ppermute | solution.py:432
  32.1 11.6 %collective-permute-start.3 = (bf16[3,2,96,256]{3,2,1,0:T(8,128)(2,1)}, bf16[3,2,96,256]{3,2,1,0:T(8,128)(2,1)S(1)}, u32[]{:S(2)}, u32[]{:S(2)}) collective-permute-start(bf16[3,2,96,256]{3,2,1,0:T(8,128)(2,1)} %bitcast.3.refs_5_), channel_id=1, source_target_pairs={{0,8},{8,0},{16,24},{24,16},{1,9},{9,1},{17,25},{25,17},{2,10},{10... | collective-permute-start | bytes 884744 | tf_op jit(solution)/shard_map/ppermute | solution.py:433
  32.3 15.2 %collective-permute-start.5 = (bf16[3,2,96,256]{3,2,1,0:T(8,128)(2,1)S(1)}, bf16[3,2,96,256]{3,2,1,0:T(8,128)(2,1)S(1)}, u32[]{:S(2)}, u32[]{:S(2)}) collective-permute-start(bf16[3,2,96,256]{3,2,1,0:T(8,128)(2,1)S(1)} %partial.3), channel_id=1, source_target_pairs={{0,16},{8,24},{1,17},{9,25},{2,18},{10,26},{3,19},{11,27},{4,20},{... | collective-permute-start | bytes 884744 | tf_op jit(solution)/shard_map/ppermute | solution.py:432
  33.6 1.2 %copy-start.8 = (bf16[1,1,3,2,80,256]{5,4,3,2,1,0:T(8,128)(2,1)S(1)}, bf16[1,1,3,2,80,256]{5,4,3,2,1,0:T(8,128)(2,1)}, u32[]{:S(2)}) copy-start(bf16[1,1,3,2,80,256]{5,4,3,2,1,0:T(8,128)(2,1)} %copy-done.7) | copy-start | bytes 737284
  33.6 3.2 %copy-start.5 = (bf16[1,2,256,256]{3,2,1,0:T(8,128)(2,1)S(1)}, bf16[1,2,256,256]{3,2,1,0:T(8,128)(2,1)}, u32[]{:S(2)}) copy-start(bf16[1,2,256,256]{3,2,1,0:T(8,128)(2,1)} %param.6) | copy-start | bytes 786436
  33.6 3.2 %copy-start.6 = (bf16[2,256,256]{2,1,0:T(8,128)(2,1)S(1)}, bf16[2,256,256]{2,1,0:T(8,128)(2,1)}, u32[]{:S(2)}) copy-start(bf16[2,256,256]{2,1,0:T(8,128)(2,1)} %get-tuple-element.35.upper) | copy-start | bytes 786436
  34.8 19.0 %collective-permute-start.15 = (bf16[3,2,80,256]{3,2,1,0:T(8,128)(2,1)S(1)}, bf16[3,2,80,256]{3,2,1,0:T(8,128)(2,1)S(1)}, u32[]{:S(2)}, u32[]{:S(2)}) collective-permute-start(bf16[3,2,80,256]{3,2,1,0:T(8,128)(2,1)S(1)} %bitcast.19), channel_id=1, source_target_pairs={{0,8},{8,0},{16,24},{24,16},{1,9},{9,1},{17,25},{25,17},{2,10},{10... | collective-permute-start | bytes 737288 | tf_op jit(solution)/shard_map/ppermute | solution.py:433
  35.5 18.3 %collective-permute-start.17 = (bf16[3,2,80,256]{3,2,1,0:T(8,128)(2,1)S(1)}, bf16[3,2,80,256]{3,2,1,0:T(8,128)(2,1)S(1)}, u32[]{:S(2)}, u32[]{:S(2)}) collective-permute-start(bf16[3,2,80,256]{3,2,1,0:T(8,128)(2,1)S(1)} %partial.5), channel_id=1, source_target_pairs={{0,16},{8,24},{1,17},{9,25},{2,18},{10,26},{3,19},{11,27},{4,20},{... | collective-permute-start | bytes 737288 | tf_op jit(solution)/shard_map/ppermute | solution.py:432
  38.2 0.9 %copy-start.4 = (bf16[1536,256]{1,0:T(8,128)(2,1)}, bf16[1536,256]{1,0:T(8,128)(2,1)S(1)}, u32[]{:S(2)}) copy-start(bf16[1536,256]{1,0:T(8,128)(2,1)S(1)} %get-tuple-element.19.refs_10_) | copy-start | bytes 2359300
  43.6 10.2 %copy-start.3 = (bf16[1,1,3,2,256,256]{5,4,3,2,1,0:T(8,128)(2,1)S(1)}, bf16[1,1,3,2,256,256]{5,4,3,2,1,0:T(8,128)(2,1)}, u32[]{:S(2)}) copy-start(bf16[1,1,3,2,256,256]{5,4,3,2,1,0:T(8,128)(2,1)} %copy-done.2) | copy-start | bytes 2359300
  43.6 16.3 %collective-permute-start.19 = (bf16[2,2,80,256]{3,2,1,0:T(8,128)(2,1)S(1)}, bf16[2,2,80,256]{3,2,1,0:T(8,128)(2,1)S(1)}, u32[]{:S(2)}, u32[]{:S(2)}) collective-permute-start(bf16[2,2,80,256]{3,2,1,0:T(8,128)(2,1)S(1)} %get-tuple-element.26), channel_id=1, source_target_pairs={{0,1},{1,0},{2,3},{3,2},{4,5},{5,4},{6,7},{7,6},{8,9},{9,8},{10,11... | collective-permute-start | bytes 491528 | tf_op jit(solution)/shard_map/ppermute | solution.py:448
  49.9 20.5 %collective-permute-start.18 = (bf16[2,2,96,256]{3,2,1,0:T(8,128)(2,1)S(1)}, bf16[2,2,96,256]{3,2,1,0:T(8,128)(2,1)S(1)}, u32[]{:S(2)}, u32[]{:S(2)}) collective-permute-start(bf16[2,2,96,256]{3,2,1,0:T(8,128)(2,1)S(1)} %get-tuple-element.25), channel_id=1, source_target_pairs={{0,1},{1,0},{2,3},{3,2},{4,5},{5,4},{6,7},{7,6},{8,9},{9,8},{10,11... | collective-permute-start | bytes 589832 | tf_op jit(solution)/shard_map/ppermute | solution.py:448
  50.0 20.4 %collective-permute-start.21 = (bf16[2,2,96,256]{3,2,1,0:T(8,128)(2,1)S(1)}, bf16[2,2,96,256]{3,2,1,0:T(8,128)(2,1)S(1)}, u32[]{:S(2)}, u32[]{:S(2)}) collective-permute-start(bf16[2,2,96,256]{3,2,1,0:T(8,128)(2,1)S(1)} %get-tuple-element.28), channel_id=1, source_target_pairs={{1,2},{3,4},{5,6},{2,1},{4,3},{6,5},{9,10},{11,12},{13,14},{10,9},... | collective-permute-start | bytes 589832 | tf_op jit(solution)/shard_map/ppermute | solution.py:449
  56.1 14.3 %collective-permute-start.20 = (bf16[2,2,80,256]{3,2,1,0:T(8,128)(2,1)S(1)}, bf16[2,2,80,256]{3,2,1,0:T(8,128)(2,1)S(1)}, u32[]{:S(2)}, u32[]{:S(2)}) collective-permute-start(bf16[2,2,80,256]{3,2,1,0:T(8,128)(2,1)S(1)} %get-tuple-element.27), channel_id=1, source_target_pairs={{0,1},{1,0},{2,3},{3,2},{4,5},{5,4},{6,7},{7,6},{8,9},{9,8},{10,11... | collective-permute-start | bytes 491528 | tf_op jit(solution)/shard_map/ppermute | solution.py:448
  56.1 14.3 %collective-permute-start.22 = (bf16[2,2,80,256]{3,2,1,0:T(8,128)(2,1)S(1)}, bf16[2,2,80,256]{3,2,1,0:T(8,128)(2,1)S(1)}, u32[]{:S(2)}, u32[]{:S(2)}) collective-permute-start(bf16[2,2,80,256]{3,2,1,0:T(8,128)(2,1)S(1)} %get-tuple-element.29), channel_id=1, source_target_pairs={{1,2},{3,4},{5,6},{2,1},{4,3},{6,5},{9,10},{11,12},{13,14},{10,9},... | collective-permute-start | bytes 491528 | tf_op jit(solution)/shard_map/ppermute | solution.py:449
  60.0 10.5 %collective-permute-start.23 = (bf16[2,2,80,256]{3,2,1,0:T(8,128)(2,1)S(1)}, bf16[2,2,80,256]{3,2,1,0:T(8,128)(2,1)S(1)}, u32[]{:S(2)}, u32[]{:S(2)}) collective-permute-start(bf16[2,2,80,256]{3,2,1,0:T(8,128)(2,1)S(1)} %get-tuple-element.30), channel_id=1, source_target_pairs={{1,2},{3,4},{5,6},{2,1},{4,3},{6,5},{9,10},{11,12},{13,14},{10,9},... | collective-permute-start | bytes 491528 | tf_op jit(solution)/shard_map/ppermute | solution.py:449

commit v2 on v1

--- a/solution.py
+++ b/solution.py
@@ -153,18 +153,19 @@
 
 
 ON_CHIP = [(0, 1), (1, 0), (2, 3), (3, 2)]
-RAW = [(2, 0), (3, 1)]
-RAW_ONE = [(3, 1)]
-PARTIAL = [(0, 2), (1, 3)]
+ACROSS = [(0, 2), (2, 0), (1, 3), (3, 1)]
+SHARES = (3, 3, 2)
 
 
 def chunks_of(rows):
+    unit = rows // 8
     if rows % 256:
         return ((0, rows),)
-    unit = rows // 16
-    sizes = (6 * unit, 5 * unit, 5 * unit)
-    starts = (0, 6 * unit, 11 * unit)
-    return tuple(zip(starts, sizes))
+    start, found = (0, [])
+    for share in SHARES:
+        found.append((start, share * unit))
+        start += share * unit
+    return tuple(found)
 
 
 def whole(shape):
@@ -198,60 +199,85 @@
     return (first[0] + second[0], first[1] + second[1])
 
 
-def partial_kernel(place, l_own, g_own, l_mate, g_mate, l_far, out):
+def pack_kernel(place, l_own, g_own, l_mate, g_mate, out):
     l_own, g_own, l_mate, g_mate = (r.at[0, 0] for r in (l_own, g_own, l_mate, g_mate))
-    bands = l_own.shape[0]
-
-    @pl.when(place[0] == 0)
-    def _():
-        for b in range(bands):
-            total = added(times_conj(l_own[b], g_own[b]), times_conj(l_mate[b], g_mate[b]))
-            out[b, 0] = total[0].astype(out.dtype)
-            out[b, 1] = total[1].astype(out.dtype)
-
-    @pl.when(place[0] == 1)
-    def _():
-        for b in range(bands):
-            total = added(times_conj(l_own[b], g_mate[b]), times_conj(l_far[b], g_own[b]))
-            out[b, 0] = total[0].astype(out.dtype)
-            out[b, 1] = total[1].astype(out.dtype)
-
-
-def polar_kernel(factor, place, l_own, g_own, l_mate, g_mate, g_far, g_far_mate, l_far, arrived,
+    rows = l_own.shape[2]
+    half = rows // 2
+
+    def put(b, total, start=0):
+        out[b, 0, start : start + total[0].shape[0]] = total[0].astype(out.dtype)
+        out[b, 1, start : start + total[1].shape[0]] = total[1].astype(out.dtype)
+
+    for b in range(l_own.shape[0]):
+
+        @pl.when(place[0] == 0)
+        def _():
+            own = times_conj(l_own[b], g_own[b])
+            put(b, added(own, times_conj(l_mate[b], g_mate[b])))
+            out[b, :, rows:] = g_mate[b, :, :half]
+
+        @pl.when(place[0] == 1)
+        def _():
+            put(b, times_conj(l_own[b], g_mate[b]))
+            out[b, :, rows:] = g_own[b, :, half:]
+
+        @pl.when(place[0] == 2)
+        def _():
+            out[b, :, :rows] = g_own[b]
+            put(b, times_conj(l_own[b, :, :half], g_mate[b, :, :half]), rows)
+
+        @pl.when(place[0] == 3)
+        def _():
+            out[b, :, :rows] = g_own[b]
+            put(b, times_conj(l_mate[b, :, half:], g_own[b, :, half:]), rows)
+
+
+def polar_kernel(factor, place, l_own, g_own, l_mate, g_mate, arrived, beside,
                  w_m1, w_0, w_1, w_2, near, far, own, polar):
     l_own, g_own, l_mate, g_mate = (r.at[0, 0] for r in (l_own, g_own, l_mate, g_mate))
     bands, _, rows, width = l_own.shape
-
-    def put(b, total):
+    half = rows // 2
+
+    def put(b, total, start=0):
+        size = total[0].shape[0]
         re = (-total[1] * factor).astype(polar.dtype)
         im = (total[0] * factor).astype(polar.dtype)
-        polar[b, :rows, :width] = re
-        polar[b, rows:, :width] = im
-        polar[b, :rows, width:] = -im
-        polar[b, rows:, width:] = re
-
-    @pl.when(place[0] == 0)
-    def _():
-        for b in range(bands):
-            put(b, added(times_conj(l_own[b], g_far[b]), times_conj(l_mate[b], g_far_mate[b])))
-
-    @pl.when(place[0] == 1)
-    def _():
-        for b in range(bands):
-            total = added(times_conj(l_mate[b], g_own[b]), times_conj(l_own[b], g_far_mate[b]))
-            put(b, added(total, times_conj(l_far[b], g_far[b])))
-
-    @pl.when(place[0] == 2)
-    def _():
-        for b in range(bands):
-            total = added(times_conj(l_own[b], g_own[b]), times_conj(l_mate[b], g_mate[b]))
-            put(b, added(total, (f32(arrived[b, 0]), f32(arrived[b, 1]))))
-
-    @pl.when(place[0] == 3)
-    def _():
-        for b in range(bands):
-            total = times_conj(l_own[b], g_mate[b])
-            put(b, added(total, (f32(arrived[b, 0]), f32(arrived[b, 1]))))
+        polar[b, start : start + size, :width] = re
+        polar[b, rows + start : rows + start + size, :width] = im
+        polar[b, start : start + size, width:] = -im
+        polar[b, rows + start : rows + start + size, width:] = re
+
+    def two(first, second):
+        return added(times_conj(*first), times_conj(*second))
+
+    def plus(total, third):
+        return added(total, (f32(third[0]), f32(third[1])))
+
+    halves = ((0, half, beside), (half, rows, arrived))
+    for b in range(bands):
+
+        @pl.when(place[0] == 0)
+        def _():
+            put(b, two((l_own[b], arrived[b, :, :rows]), (l_mate[b], beside[b, :, :rows])))
+
+        @pl.when(place[0] == 1)
+        def _():
+            for low, high, extra in halves:
+                cut = (b, slice(None), slice(low, high))
+                total = two((l_mate[cut], g_own[cut]), (l_own[cut], beside[cut]))
+                put(b, plus(total, extra[b, :, rows:]), low)
+
+        @pl.when(place[0] == 2)
+        def _():
+            total = two((l_own[b], g_own[b]), (l_mate[b], g_mate[b]))
+            put(b, plus(total, arrived[b, :, :rows]))
+
+        @pl.when(place[0] == 3)
+        def _():
+            for low, high, extra in halves:
+                cut = (b, slice(None), slice(low, high))
+                total = two((l_mate[cut], extra[b, :, rows:]), (l_own[cut], g_mate[cut]))
+                put(b, plus(total, arrived[cut]), low)
 
     def product(bands_used, weights):
         total = None
@@ -292,6 +318,12 @@
     core = place[2]
     even = place[1] == 0
 
+    own_kept = (place[3] == 0).astype(diag.dtype)
+    above_kept = (place[4] == 0).astype(diag.dtype)
+
+    def kept(block, factor):
+        return (block[0] * factor, block[1] * factor)
+
     def adjoint(block):
         return (block[0].T, -(block[1].T))
 
@@ -307,7 +339,7 @@
         left[width:, base + width : base + 2 * width] = block[0]
 
     def work(diag_near, upper_near, diag_far, upper_far):
-        own = (upper[0], upper[1])
+        own = kept(upper, own_kept)
         own_adjoint = adjoint(own)
         put(w_0, 1, diag)
         put(w_0, 2, own_adjoint)
@@ -321,7 +353,7 @@
             put(w_m1, 1, below_adjoint)
             put(w_0, 0, below)
             put(w_1, 1, diag_above)
-            put(w_2, 0, upper_above)
+            put(w_2, 0, kept(upper_above, above_kept))
             put_left(below_at, below_adjoint)
             put_left(above_at, own)
 
@@ -373,6 +405,10 @@
         out[...] = total.astype(out.dtype).reshape(2, width, width)
 
 
+def called(kernel, *args, **kwargs):
+    return pl.pallas_call(kernel, grid=(1,), compiler_params=params(), **kwargs)(*args)
+
+
 def exchanged(g_lesser, g_greater, v_diag, v_upper):
     bf16 = jnp.bfloat16
     energies = lax.axis_size("energy")
@@ -381,78 +417,67 @@
     energy = lax.axis_index("energy")
     slab = lax.axis_index("slab")
     core = energy % 2
-    place = jnp.stack([energy, slab % 2, core]).astype(jnp.int32)
+    place = jnp.stack([energy, slab % 2, core, slab == slabs - 1, slab == slabs - 2])
+    place = place.astype(jnp.int32)
     near_pairs = [(i, i ^ 1) for i in range(slabs)]
     far_pairs = [(i, i + 1) for i in range(1, slabs - 1, 2)]
     far_pairs = far_pairs + [(j, i) for i, j in far_pairs]
+    chunks = chunks_of(width)
 
     l_own, g_own = g_lesser, g_greater
     l_mate = lax.ppermute(l_own, "energy", ON_CHIP)
     g_mate = lax.ppermute(g_own, "energy", ON_CHIP)
 
-    upper = jnp.where(slab == slabs - 1, jnp.zeros_like(v_upper), v_upper)[0]
-    diag = v_diag[0]
+    diag, upper = v_diag[0], v_upper[0]
     sent = jnp.where(core == 0, diag, upper)
     v_near = lax.ppermute(sent, "slab", near_pairs)
     v_far = lax.ppermute(sent, "slab", far_pairs)
     v_near_mate = lax.ppermute(v_near, "energy", ON_CHIP)
     v_far_mate = lax.ppermute(v_far, "energy", ON_CHIP)
     square = (2, width, width)
-    right = [
-        jax.ShapeDtypeStruct((2 * width * n, width), bf16) for n in (2, 3, 2, 1)
-    ]
-    *rights, left = pl.pallas_call(
+    right = [jax.ShapeDtypeStruct((2 * width * n, width), bf16) for n in (2, 3, 2, 1)]
+    *rights, left = called(
         coupling_kernel,
+        place, diag, upper, v_near, v_near_mate, v_far, v_far_mate,
         out_shape=(*right, jax.ShapeDtypeStruct((2 * width, 6 * width), bf16)),
         in_specs=[scalars()] + [whole(square)] * 6,
         out_specs=tuple(whole(r.shape) for r in right) + (whole((2 * width, 6 * width)),),
-        compiler_params=params(),
-        grid=(1,),
-        name="coupling",
-    )(place, diag, upper, v_near, v_near_mate, v_far, v_far_mate)
+    )
 
     owns, nears, fars = [], [], []
-    for start, size in chunks_of(width):
-        def cut(value):
-            return lax.slice_in_dim(value, start, start + size, axis=4)
-
-        piece = (bands, 2, size, width)
-        raw_g = lax.ppermute(cut(g_own), "energy", RAW).reshape(piece)
-        raw_l = lax.ppermute(cut(l_mate), "energy", RAW_ONE).reshape(piece)
+    for start, size in chunks:
+        payload = (bands, 2, size + size // 2, width)
         rows = rows_of(g_own.shape, start, size)
-        partial = pl.pallas_call(
-            partial_kernel,
-            out_shape=jax.ShapeDtypeStruct(piece, bf16),
-            in_specs=[scalars()] + [rows] * 4 + [whole(piece)],
-            out_specs=whole(piece),
-            compiler_params=params(),
-            grid=(1,),
-        name="partial",
-        )(place, l_own, g_own, l_mate, g_mate, raw_l)
-        arrived = lax.ppermute(partial, "energy", PARTIAL)
-        raw_g_mate = lax.ppermute(raw_g, "energy", ON_CHIP)
+        packed = called(
+            pack_kernel,
+            place, l_own, g_own, l_mate, g_mate,
+            out_shape=jax.ShapeDtypeStruct(payload, bf16),
+            in_specs=[scalars()] + [rows] * 4,
+            out_specs=whole(payload),
+        )
+        arrived = lax.ppermute(packed, "energy", ACROSS)
+        beside = lax.ppermute(arrived, "energy", ON_CHIP)
         term = (2, 2, size, width)
-        near, far, own = pl.pallas_call(
+        near, far, own = called(
             lambda *refs: polar_kernel(1.0 / math.sqrt(energies), *refs),
+            place, l_own, g_own, l_mate, g_mate, arrived, beside, *rights,
             out_shape=(jax.ShapeDtypeStruct(term, bf16),) * 3,
             in_specs=[scalars()]
             + [rows] * 4
-            + [whole(piece)] * 4
+            + [whole(payload)] * 2
             + [whole(r.shape) for r in right],
             out_specs=(whole(term),) * 3,
             scratch_shapes=[pltpu.VMEM((bands, 2 * size, 2 * width), bf16)],
-            compiler_params=params(),
-            grid=(1,),
-        name="polar",
-        )(place, l_own, g_own, l_mate, g_mate, raw_g, raw_g_mate, raw_l, arrived, *rights)
+        )
         nears.append(lax.ppermute(near, "slab", near_pairs))
         fars.append(lax.ppermute(far, "slab", far_pairs))
         owns.append(own)
 
     count = len(owns)
     anywhere = pl.BlockSpec(memory_space=pl.ANY)
-    w_diag, w_upper = pl.pallas_call(
+    w_diag, w_upper = called(
         lambda *refs: final_kernel(count, *refs),
+        *owns, *nears, *fars, left,
         out_shape=(jax.ShapeDtypeStruct(square, bf16),) * 2,
         in_specs=[anywhere] * (3 * count) + [whole((2 * width, 6 * width))],
         out_specs=(whole(square),) * 2,
@@ -460,19 +485,17 @@
             pltpu.VMEM((3, 2, 2, width, width), bf16),
             pltpu.SemaphoreType.DMA((3, count)),
         ],
-        compiler_params=params(),
-        grid=(1,),
-        name="final",
-    )(*owns, *nears, *fars, left)
+    )
     shape = (1, 1) + square
     return w_diag.reshape(shape), w_upper.reshape(shape)
 
 
+def fast(mesh):
+    return mesh.shape["energy"] == 4 and mesh.shape["slab"] % 2 == 0
+
+
 def per_device(g_lesser, g_greater, v_diag, v_upper):
-    paired = lax.axis_size("energy") == 4 and lax.axis_size("slab") % 2 == 0
-    if paired and g_lesser.shape[0] == 1 and v_diag.shape[0] == 1:
-        return exchanged(g_lesser, g_greater, v_diag, v_upper)
-    return general(g_lesser, g_greater, v_diag, v_upper)
+    return exchanged(g_lesser, g_greater, v_diag, v_upper)
 
 
 def solution(mesh):
@@ -482,8 +505,9 @@
         P("slab", None, None, None),
         P("slab", None, None, None),
     )
+    quick = fast(mesh)
     return jax.shard_map(
-        per_device,
+        per_device if quick else general,
         mesh=mesh,
         in_specs=placed,
         out_specs=(P("energy", "slab", None, None, None), P("energy", "slab", None, None, None)),

time: 73.4 us -> 71.4 us (0.973)
  waiting for transfers between devices: 17.7 us -> 32.3 us
  starting transfers between devices: 34.3 us -> 20.8 us
  other arithmetic: 1.92 us -> 0.03 us
  local copies, waits for them, and re-layouts: 4.35 us -> 3.25 us
    ppermute x12 -> x6, starting transfers between devices: 17.7 us -> 3.03 us  [the longest x3 3.02 us: exchanged(): arrived = lax.ppermute(packed, 'energy', ACROSS)]
    ppermute x12 -> x6, waiting for transfers between devices: 10.2 us -> 19.1 us  [the longest x3 19.1 us: exchanged(): arrived = lax.ppermute(packed, 'energy', ACROSS)]
    ppermute x3, waiting for transfers between devices: 0.01 us -> 6.93 us  [exchanged(): fars.append(lax.ppermute(far, 'slab', far_pairs))]
    ppermute x3, waiting for transfers between devices: 7.49 us -> 1.57 us  [exchanged(): nears.append(lax.ppermute(near, 'slab', near_pairs))]
    ppermute x3, starting transfers between devices: 0.21 us -> 3.73 us  [exchanged(): nears.append(lax.ppermute(near, 'slab', near_pairs))]
    slice x4 -> x0, local copies, waits for them, and re-layouts: 3.42 us -> none  [cut(): return lax.slice_in_dim(value, start, start + size, axis=4)]
    unnamed x18 -> x14, local copies, waits for them, and re-layouts: 0.92 us -> 3.17 us
    ppermute x1, waiting for transfers between devices: 0.01 us -> 1.9 us  [exchanged(): l_mate = lax.ppermute(l_own, 'energy', ON_CHIP)]
  transfers between devices with their start and end apart: 24 -> 18, of which waited for: 5 -> 9; matrix products, arithmetic and copies ran while one was open for 7% -> 0% of each run, Pallas kernels for 15% -> 14%
where the time goes in v2:
time: 71.4 us; the launch traced here: 71 us
  waiting for transfers between devices  32.3 us (45%)
  starting transfers between devices  20.8 us (29%)
  Pallas kernels  13.8 us (19%)
  local copies, waits for them, and re-layouts  3.25 us (5%)
  between operations  0.76 us (1%)
    ppermute x3, waiting for transfers between devices, exchanged(): arrived = lax.ppermute(packed, 'energy', ACROSS)  19.1 us
    pallas_call x8, Pallas kernels, called(): pl.pallas_call(kernel, grid=(1,), compiler_params=params(), **kwargs)(*args)  13.8 us
    ppermute x3, starting transfers between devices, exchanged(): fars.append(lax.ppermute(far, 'slab', far_pairs))  9.04 us
    ppermute x3, waiting for transfers between devices, exchanged(): fars.append(lax.ppermute(far, 'slab', far_pairs))  6.93 us
    ppermute x3, starting transfers between devices, exchanged(): nears.append(lax.ppermute(near, 'slab', near_pairs))  3.73 us
    unnamed x14, local copies, waits for them, and re-layouts  3.17 us
    ppermute x3, starting transfers between devices, exchanged(): arrived = lax.ppermute(packed, 'energy', ACROSS)  3.02 us
    ppermute x1, starting transfers between devices, exchanged(): v_far = lax.ppermute(sent, 'slab', far_pairs)  2.29 us
  transfers between devices with their start and end apart: 18, of which 9 were waited for; matrix products, arithmetic and copies ran while one was open for 0% of the time, Pallas kernels for 14%

profile of v2, /device:TPU:26, one launch (start us, length us, event | category | flops | bytes accessed | tf_op | source)
XLA Modules:
  0.0 71.0 jit_solution(14313100869469824577)
XLA Ops:
  0.6 0.1 collective-permute-start
  0.7 0.5 collective-permute-start.1
  1.2 0.1 stack.31.place.refs_0_
  1.3 1.9 %collective-permute-done.l_mate.refs_3_ = bf16[1,1,3,2,256,256]{5,4,3,2,1,0:T(8,128)(2,1)S(1)} collective-permute-done((bf16[1,1,3,2,256,256]{5,4,3,2,1,0:T(8,128)(2,1)}, bf16[1,1,3,2,256,256]{5,4,3,2,1,0:T(8,128)(2,1)S(1)}, u32[]{:S(2)}, u32[]{:S(2)}) %collective-permute-start) | collective-permute-done | bytes 786464 | tf_op jit(solution)/shard_map/ppermute | solution.py:428
  3.2 1.1 %collective-permute-done.1.g_mate.refs_4_ = bf16[1,1,3,2,256,256]{5,4,3,2,1,0:T(8,128)(2,1)S(1)} collective-permute-done((bf16[1,1,3,2,256,256]{5,4,3,2,1,0:T(8,128)(2,1)}, bf16[1,1,3,2,256,256]{5,4,3,2,1,0:T(8,128)(2,1)S(1)}, u32[]{:S(2)}, u32[]{:S(2)}) %collective-permute-start.1) | collective-permute-done | bytes 786464 | tf_op jit(solution)/shard_map/ppermute | solution.py:429
  4.3 1.1 %copy-done = bf16[1,1,3,2,256,256]{5,4,3,2,1,0:T(8,128)(2,1)S(1)} copy-done((bf16[1,1,3,2,256,256]{5,4,3,2,1,0:T(8,128)(2,1)S(1)}, bf16[1,1,3,2,256,256]{5,4,3,2,1,0:T(8,128)(2,1)}, u32[]{:S(2)}) %copy-start) | copy-done | bytes 786456
  5.5 1.1 %copy-done.2 = bf16[1,1,3,2,256,256]{5,4,3,2,1,0:T(8,128)(2,1)S(1)} copy-done((bf16[1,1,3,2,256,256]{5,4,3,2,1,0:T(8,128)(2,1)S(1)}, bf16[1,1,3,2,256,256]{5,4,3,2,1,0:T(8,128)(2,1)}, u32[]{:S(2)}) %copy-start.2) | copy-done | bytes 786456
  6.6 1.5 %shard_map.59 = bf16[3,2,144,256]{3,2,1,0:T(8,128)(2,1)} custom-call(s32[5]{0:T(128)S(1)} %stack.31.place.refs_0_, bf16[1,1,3,2,256,256]{5,4,3,2,1,0:T(8,128)(2,1)S(1)} %copy-done, bf16[1,1,3,2,256,256]{5,4,3,2,1,0:T(8,128)(2,1)S(1)} %copy-done.2, bf16[1,1,3,2,256,256]{5,4,3,2,1,0:T(8,128)(2,1)S(1)} %collective-permute-done.l_mate.refs_3_, ...), custom_call_target="tpu_custom_call" | custom-call | tf_op jit(solution)/shard_map/pallas_call | solution.py:409
  8.1 0.8 %collective-permute-start.2 = (bf16[3,2,144,256]{3,2,1,0:T(8,128)(2,1)}, bf16[3,2,144,256]{3,2,1,0:T(8,128)(2,1)}, u32[]{:S(2)}, u32[]{:S(2)}) collective-permute-start(bf16[3,2,144,256]{3,2,1,0:T(8,128)(2,1)} %shard_map.59), channel_id=1, source_target_pairs={{0,16},{16,0},{8,24},{24,8},{1,17},{17,1},{9,25},{25,9},{2,18},{18... | collective-permute-start | bytes 1327112 | tf_op jit(solution)/shard_map/ppermute | solution.py:458
  8.9 1.5 %shard_map.62 = bf16[3,2,144,256]{3,2,1,0:T(8,128)(2,1)} custom-call(s32[5]{0:T(128)S(1)} %stack.31.place.refs_0_, bf16[1,1,3,2,256,256]{5,4,3,2,1,0:T(8,128)(2,1)S(1)} %copy-done, bf16[1,1,3,2,256,256]{5,4,3,2,1,0:T(8,128)(2,1)S(1)} %copy-done.2, bf16[1,1,3,2,256,256]{5,4,3,2,1,0:T(8,128)(2,1)S(1)} %collective-permute-done.l_mate.refs_3_, ...), custom_call_target="tpu_custom_call" | custom-call | tf_op jit(solution)/shard_map/pallas_call | solution.py:409
  10.3 1.5 %collective-permute-start.8 = (bf16[3,2,144,256]{3,2,1,0:T(8,128)(2,1)}, bf16[3,2,144,256]{3,2,1,0:T(8,128)(2,1)}, u32[]{:S(2)}, u32[]{:S(2)}) collective-permute-start(bf16[3,2,144,256]{3,2,1,0:T(8,128)(2,1)} %shard_map.62), channel_id=1, source_target_pairs={{0,16},{16,0},{8,24},{24,8},{1,17},{17,1},{9,25},{25,9},{2,18},{18... | collective-permute-start | bytes 1327112 | tf_op jit(solution)/shard_map/ppermute | solution.py:458
  11.8 0.7 shard_map.64
  12.5 0.8 %collective-permute-start.10 = (bf16[3,2,96,256]{3,2,1,0:T(8,128)(2,1)S(1)}, bf16[3,2,96,256]{3,2,1,0:T(8,128)(2,1)S(1)}, u32[]{:S(2)}, u32[]{:S(2)}) collective-permute-start(bf16[3,2,96,256]{3,2,1,0:T(8,128)(2,1)S(1)} %shard_map.64), channel_id=1, source_target_pairs={{0,16},{16,0},{8,24},{24,8},{1,17},{17,1},{9,25},{25,9},{2,18},{18... | collective-permute-start | bytes 884744 | tf_op jit(solution)/shard_map/ppermute | solution.py:458
  13.3 1.6 %collective-permute-start.4 = (bf16[2,256,256]{2,1,0:T(8,128)(2,1)S(1)}, bf16[2,256,256]{2,1,0:T(8,128)(2,1)S(1)}, u32[]{:S(2)}, u32[]{:S(2)}) collective-permute-start(bf16[2,256,256]{2,1,0:T(8,128)(2,1)S(1)} %broadcast_select_fusion), channel_id=1, source_target_pairs={{0,1},{1,0},{2,3},{3,2},{4,5},{5,4},{6,7},{7,6},{8,9},{9,8},{10,11... | collective-permute-start | bytes 786440 | tf_op jit(solution)/shard_map/ppermute | solution.py:433
  14.9 2.3 %collective-permute-start.6 = (bf16[2,256,256]{2,1,0:T(8,128)(2,1)S(1)}, bf16[2,256,256]{2,1,0:T(8,128)(2,1)S(1)}, u32[]{:S(2)}, u32[]{:S(2)}) collective-permute-start(bf16[2,256,256]{2,1,0:T(8,128)(2,1)S(1)} %broadcast_select_fusion), channel_id=1, source_target_pairs={{1,2},{3,4},{5,6},{2,1},{4,3},{6,5},{9,10},{11,12},{13,14},{10,9},... | collective-permute-start | bytes 786440 | tf_op jit(solution)/shard_map/ppermute | solution.py:434
  17.2 4.2 %collective-permute-done.2.refs_5_ = bf16[3,2,144,256]{3,2,1,0:T(8,128)(2,1)} collective-permute-done((bf16[3,2,144,256]{3,2,1,0:T(8,128)(2,1)}, bf16[3,2,144,256]{3,2,1,0:T(8,128)(2,1)}, u32[]{:S(2)}, u32[]{:S(2)}) %collective-permute-start.2) | collective-permute-done | bytes 442400 | tf_op jit(solution)/shard_map/ppermute | solution.py:458
  21.4 0.0 collective-permute-start.3
  21.4 9.5 %collective-permute-done.8.refs_5_ = bf16[3,2,144,256]{3,2,1,0:T(8,128)(2,1)} collective-permute-done((bf16[3,2,144,256]{3,2,1,0:T(8,128)(2,1)}, bf16[3,2,144,256]{3,2,1,0:T(8,128)(2,1)}, u32[]{:S(2)}, u32[]{:S(2)}) %collective-permute-start.8) | collective-permute-done | bytes 442400 | tf_op jit(solution)/shard_map/ppermute | solution.py:458
  30.9 0.0 collective-permute-start.9
  30.9 5.4 %collective-permute-done.10.refs_5_ = bf16[3,2,96,256]{3,2,1,0:T(8,128)(2,1)S(1)} collective-permute-done((bf16[3,2,96,256]{3,2,1,0:T(8,128)(2,1)S(1)}, bf16[3,2,96,256]{3,2,1,0:T(8,128)(2,1)S(1)}, u32[]{:S(2)}, u32[]{:S(2)}) %collective-permute-start.10) | collective-permute-done | bytes 294944 | tf_op jit(solution)/shard_map/ppermute | solution.py:458
  36.3 0.0 collective-permute-start.11
  36.3 0.0 collective-permute-done.4.near
  36.3 0.5 collective-permute-start.5
  36.8 0.0 collective-permute-done.6.far
  36.8 0.1 collective-permute-start.7
  36.9 1.4 %collective-permute-done.5.near_mate = bf16[2,256,256]{2,1,0:T(8,128)(2,1)S(1)} collective-permute-done((bf16[2,256,256]{2,1,0:T(8,128)(2,1)S(1)}, bf16[2,256,256]{2,1,0:T(8,128)(2,1)S(1)}, u32[]{:S(2)}, u32[]{:S(2)}) %collective-permute-start.5) | collective-permute-done | bytes 262176 | tf_op jit(solution)/shard_map/ppermute | solution.py:435
  38.3 0.4 collective-permute-done.7.far_mate
  38.6 0.9 %shard_map.60 = (bf16[1024,256]{1,0:T(8,128)(2,1)S(1)}, bf16[1536,256]{1,0:T(8,128)(2,1)S(1)}, bf16[1024,256]{1,0:T(8,128)(2,1)S(1)}, bf16[512,256]{1,0:T(8,128)(2,1)S(1)}, bf16[512,1536]{1,0:T(8,128)(2,1)S(1)}) custom-call(s32[5]{0:T(128)S(1)} %stack.31.place.refs_0_, bf16[2,256,256]{2,1,0:T(8,128)(2,1)S(1)} %bitcast.11, bf16[2,256,256]{2,1,0:T(8,128)(2,1)S(1)} %bitcast.12, ...), custom_call_target="tpu_custom_call" | custom-call | tf_op jit(solution)/shard_map/pallas_call | solution.py:409
  39.5 0.9 %copy-done.4 = bf16[1536,256]{1,0:T(8,128)(2,1)} copy-done((bf16[1536,256]{1,0:T(8,128)(2,1)}, bf16[1536,256]{1,0:T(8,128)(2,1)S(1)}, u32[]{:S(2)}) %copy-start.4) | copy-done | bytes 786456
  40.4 0.0 collective-permute-done.11.refs_6_
  40.4 2.0 %shard_map.65 = (bf16[2,2,64,256]{3,2,1,0:T(8,128)(2,1)S(1)}, bf16[2,2,64,256]{3,2,1,0:T(8,128)(2,1)S(1)}, bf16[2,2,64,256]{3,2,1,0:T(8,128)(2,1)S(1)}) custom-call(s32[5]{0:T(128)S(1)} %stack.31.place.refs_0_, bf16[1,1,3,2,256,256]{5,4,3,2,1,0:T(8,128)(2,1)S(1)} %copy-done.1, bf16[1,1,3,2,256,256]{5,4,3,2,1,0:T(8,128)(2,1)S(1)} %copy-done.3, ...), custom_call_target="tpu_custom_call" | custom-call | tf_op jit(solution)/shard_map/pallas_call | solution.py:409
  42.4 1.6 %collective-permute-start.14 = (bf16[2,2,64,256]{3,2,1,0:T(8,128)(2,1)S(1)}, bf16[2,2,64,256]{3,2,1,0:T(8,128)(2,1)S(1)}, u32[]{:S(2)}, u32[]{:S(2)}) collective-permute-start(bf16[2,2,64,256]{3,2,1,0:T(8,128)(2,1)S(1)} %get-tuple-element.27), channel_id=1, source_target_pairs={{0,1},{1,0},{2,3},{3,2},{4,5},{5,4},{6,7},{7,6},{8,9},{9,8},{10,11... | collective-permute-start | bytes 393224 | tf_op jit(solution)/shard_map/ppermute | solution.py:472
  44.0 0.0 collective-permute-done.3.refs_6_
  44.0 2.4 %shard_map.61 = (bf16[2,2,96,256]{3,2,1,0:T(8,128)(2,1)S(1)}, bf16[2,2,96,256]{3,2,1,0:T(8,128)(2,1)S(1)}, bf16[2,2,96,256]{3,2,1,0:T(8,128)(2,1)S(1)}) custom-call(s32[5]{0:T(128)S(1)} %stack.31.place.refs_0_, bf16[1,1,3,2,256,256]{5,4,3,2,1,0:T(8,128)(2,1)S(1)} %copy-done.1, bf16[1,1,3,2,256,256]{5,4,3,2,1,0:T(8,128)(2,1)S(1)} %copy-done.3, ...), custom_call_target="tpu_custom_call" | custom-call | tf_op jit(solution)/shard_map/pallas_call | solution.py:409
  46.5 0.6 collective-permute-start.12
  47.0 0.0 collective-permute-done.9.refs_6_
  47.0 2.4 %shard_map.63 = (bf16[2,2,96,256]{3,2,1,0:T(8,128)(2,1)S(1)}, bf16[2,2,96,256]{3,2,1,0:T(8,128)(2,1)S(1)}, bf16[2,2,96,256]{3,2,1,0:T(8,128)(2,1)S(1)}) custom-call(s32[5]{0:T(128)S(1)} %stack.31.place.refs_0_, bf16[1,1,3,2,256,256]{5,4,3,2,1,0:T(8,128)(2,1)S(1)} %copy-done.1, bf16[1,1,3,2,256,256]{5,4,3,2,1,0:T(8,128)(2,1)S(1)} %copy-done.3, ...), custom_call_target="tpu_custom_call" | custom-call | tf_op jit(solution)/shard_map/pallas_call | solution.py:409
  49.5 1.6 %collective-permute-start.13 = (bf16[2,2,96,256]{3,2,1,0:T(8,128)(2,1)S(1)}, bf16[2,2,96,256]{3,2,1,0:T(8,128)(2,1)S(1)}, u32[]{:S(2)}, u32[]{:S(2)}) collective-permute-start(bf16[2,2,96,256]{3,2,1,0:T(8,128)(2,1)S(1)} %get-tuple-element.26), channel_id=1, source_target_pairs={{0,1},{1,0},{2,3},{3,2},{4,5},{5,4},{6,7},{7,6},{8,9},{9,8},{10,11... | collective-permute-start | bytes 589832 | tf_op jit(solution)/shard_map/ppermute | solution.py:472
  51.1 2.3 %collective-permute-start.15 = (bf16[2,2,96,256]{3,2,1,0:T(8,128)(2,1)S(1)}, bf16[2,2,96,256]{3,2,1,0:T(8,128)(2,1)S(1)}, u32[]{:S(2)}, u32[]{:S(2)}) collective-permute-start(bf16[2,2,96,256]{3,2,1,0:T(8,128)(2,1)S(1)} %get-tuple-element.28), channel_id=1, source_target_pairs={{1,2},{3,4},{5,6},{2,1},{4,3},{6,5},{9,10},{11,12},{13,14},{10,9},... | collective-permute-start | bytes 589832 | tf_op jit(solution)/shard_map/ppermute | solution.py:473
  53.4 4.4 %collective-permute-start.16 = (bf16[2,2,96,256]{3,2,1,0:T(8,128)(2,1)S(1)}, bf16[2,2,96,256]{3,2,1,0:T(8,128)(2,1)S(1)}, u32[]{:S(2)}, u32[]{:S(2)}) collective-permute-start(bf16[2,2,96,256]{3,2,1,0:T(8,128)(2,1)S(1)} %get-tuple-element.29), channel_id=1, source_target_pairs={{1,2},{3,4},{5,6},{2,1},{4,3},{6,5},{9,10},{11,12},{13,14},{10,9},... | collective-permute-start | bytes 589832 | tf_op jit(solution)/shard_map/ppermute | solution.py:473
  57.8 0.0 collective-permute-done.14.refs_5_
  57.8 2.3 %collective-permute-start.17 = (bf16[2,2,64,256]{3,2,1,0:T(8,128)(2,1)S(1)}, bf16[2,2,64,256]{3,2,1,0:T(8,128)(2,1)S(1)}, u32[]{:S(2)}, u32[]{:S(2)}) collective-permute-start(bf16[2,2,64,256]{3,2,1,0:T(8,128)(2,1)S(1)} %get-tuple-element.30), channel_id=1, source_target_pairs={{1,2},{3,4},{5,6},{2,1},{4,3},{6,5},{9,10},{11,12},{13,14},{10,9},... | collective-permute-start | bytes 393224 | tf_op jit(solution)/shard_map/ppermute | solution.py:473
  60.1 6.9 %collective-permute-done.17.refs_8_ = bf16[2,2,64,256]{3,2,1,0:T(8,128)(2,1)S(1)} collective-permute-done((bf16[2,2,64,256]{3,2,1,0:T(8,128)(2,1)S(1)}, bf16[2,2,64,256]{3,2,1,0:T(8,128)(2,1)S(1)}, u32[]{:S(2)}, u32[]{:S(2)}) %collective-permute-start.17) | collective-permute-done | bytes 131104 | tf_op jit(solution)/shard_map/ppermute | solution.py:473
  67.1 0.0 collective-permute-done.12.refs_3_
  67.1 1.6 %collective-permute-done.13.refs_4_ = bf16[2,2,96,256]{3,2,1,0:T(8,128)(2,1)S(1)} collective-permute-done((bf16[2,2,96,256]{3,2,1,0:T(8,128)(2,1)S(1)}, bf16[2,2,96,256]{3,2,1,0:T(8,128)(2,1)S(1)}, u32[]{:S(2)}, u32[]{:S(2)}) %collective-permute-start.13) | collective-permute-done | bytes 196640 | tf_op jit(solution)/shard_map/ppermute | solution.py:472
  68.6 0.0 collective-permute-done.15.refs_6_
  68.6 0.0 collective-permute-done.16.refs_7_
  68.6 2.4 %shard_map.66 = (bf16[2,256,256]{2,1,0:T(8,128)(2,1)}, bf16[2,256,256]{2,1,0:T(8,128)(2,1)}) custom-call(bf16[2,2,96,256]{3,2,1,0:T(8,128)(2,1)S(1)} %get-tuple-element.22.refs_0_, bf16[2,2,96,256]{3,2,1,0:T(8,128)(2,1)S(1)} %get-tuple-element.23.refs_1_, bf16[2,2,64,256]{3,2,1,0:T(8,128)(2,1)S(1)} %get-tuple-element.24.refs_2_, ...), custom_call_target="tpu_custom_call" | custom-call | tf_op jit(solution)/shard_map/pallas_call | solution.py:409
  (12 shorter events, 0.0 us)
Async XLA Ops:
  0.6 2.6 %collective-permute-start = (bf16[1,1,3,2,256,256]{5,4,3,2,1,0:T(8,128)(2,1)}, bf16[1,1,3,2,256,256]{5,4,3,2,1,0:T(8,128)(2,1)S(1)}, u32[]{:S(2)}, u32[]{:S(2)}) collective-permute-start(bf16[1,1,3,2,256,256]{5,4,3,2,1,0:T(8,128)(2,1)} %refs_1_.5), channel_id=1, source_target_pairs={{0,8},{8,0},{16,24},{24,16},{1,9},{9,1},{17,25},{25,17},{2,10},{10... | collective-permute-start | bytes 2359304 | tf_op jit(solution)/shard_map/ppermute | solution.py:428
  0.7 3.6 %collective-permute-start.1 = (bf16[1,1,3,2,256,256]{5,4,3,2,1,0:T(8,128)(2,1)}, bf16[1,1,3,2,256,256]{5,4,3,2,1,0:T(8,128)(2,1)S(1)}, u32[]{:S(2)}, u32[]{:S(2)}) collective-permute-start(bf16[1,1,3,2,256,256]{5,4,3,2,1,0:T(8,128)(2,1)} %refs_2_.5), channel_id=1, source_target_pairs={{0,8},{8,0},{16,24},{24,16},{1,9},{9,1},{17,25},{25,17},{2,10},{10... | collective-permute-start | bytes 2359304 | tf_op jit(solution)/shard_map/ppermute | solution.py:429
  4.3 1.1 %copy-start = (bf16[1,1,3,2,256,256]{5,4,3,2,1,0:T(8,128)(2,1)S(1)}, bf16[1,1,3,2,256,256]{5,4,3,2,1,0:T(8,128)(2,1)}, u32[]{:S(2)}) copy-start(bf16[1,1,3,2,256,256]{5,4,3,2,1,0:T(8,128)(2,1)} %refs_1_.5) | copy-start | bytes 2359300
  5.4 1.1 %copy-start.2 = (bf16[1,1,3,2,256,256]{5,4,3,2,1,0:T(8,128)(2,1)S(1)}, bf16[1,1,3,2,256,256]{5,4,3,2,1,0:T(8,128)(2,1)}, u32[]{:S(2)}) copy-start(bf16[1,1,3,2,256,256]{5,4,3,2,1,0:T(8,128)(2,1)} %refs_2_.5) | copy-start | bytes 2359300
  8.1 3.8 %copy-start.1 = (bf16[1,1,3,2,256,256]{5,4,3,2,1,0:T(8,128)(2,1)S(1)}, bf16[1,1,3,2,256,256]{5,4,3,2,1,0:T(8,128)(2,1)}, u32[]{:S(2)}) copy-start(bf16[1,1,3,2,256,256]{5,4,3,2,1,0:T(8,128)(2,1)} %refs_1_.5) | copy-start | bytes 2359300
  8.1 3.8 %copy-start.3 = (bf16[1,1,3,2,256,256]{5,4,3,2,1,0:T(8,128)(2,1)S(1)}, bf16[1,1,3,2,256,256]{5,4,3,2,1,0:T(8,128)(2,1)}, u32[]{:S(2)}) copy-start(bf16[1,1,3,2,256,256]{5,4,3,2,1,0:T(8,128)(2,1)} %refs_2_.5) | copy-start | bytes 2359300
  8.1 13.4 %collective-permute-start.2 = (bf16[3,2,144,256]{3,2,1,0:T(8,128)(2,1)}, bf16[3,2,144,256]{3,2,1,0:T(8,128)(2,1)}, u32[]{:S(2)}, u32[]{:S(2)}) collective-permute-start(bf16[3,2,144,256]{3,2,1,0:T(8,128)(2,1)} %shard_map.59), channel_id=1, source_target_pairs={{0,16},{16,0},{8,24},{24,8},{1,17},{17,1},{9,25},{25,9},{2,18},{18... | collective-permute-start | bytes 1327112 | tf_op jit(solution)/shard_map/ppermute | solution.py:458
  10.3 20.6 %collective-permute-start.8 = (bf16[3,2,144,256]{3,2,1,0:T(8,128)(2,1)}, bf16[3,2,144,256]{3,2,1,0:T(8,128)(2,1)}, u32[]{:S(2)}, u32[]{:S(2)}) collective-permute-start(bf16[3,2,144,256]{3,2,1,0:T(8,128)(2,1)} %shard_map.62), channel_id=1, source_target_pairs={{0,16},{16,0},{8,24},{24,8},{1,17},{17,1},{9,25},{25,9},{2,18},{18... | collective-permute-start | bytes 1327112 | tf_op jit(solution)/shard_map/ppermute | solution.py:458
  11.8 1.5 %copy-start.5 = (bf16[1,2,256,256]{3,2,1,0:T(8,128)(2,1)S(1)}, bf16[1,2,256,256]{3,2,1,0:T(8,128)(2,1)}, u32[]{:S(2)}) copy-start(bf16[1,2,256,256]{3,2,1,0:T(8,128)(2,1)} %param.6) | copy-start | bytes 786436
  11.8 1.5 %copy-start.6 = (bf16[1,2,256,256]{3,2,1,0:T(8,128)(2,1)S(1)}, bf16[1,2,256,256]{3,2,1,0:T(8,128)(2,1)}, u32[]{:S(2)}) copy-start(bf16[1,2,256,256]{3,2,1,0:T(8,128)(2,1)} %param.7) | copy-start | bytes 786436
  12.5 23.8 %collective-permute-start.10 = (bf16[3,2,96,256]{3,2,1,0:T(8,128)(2,1)S(1)}, bf16[3,2,96,256]{3,2,1,0:T(8,128)(2,1)S(1)}, u32[]{:S(2)}, u32[]{:S(2)}) collective-permute-start(bf16[3,2,96,256]{3,2,1,0:T(8,128)(2,1)S(1)} %shard_map.64), channel_id=1, source_target_pairs={{0,16},{16,0},{8,24},{24,8},{1,17},{17,1},{9,25},{25,9},{2,18},{18... | collective-permute-start | bytes 884744 | tf_op jit(solution)/shard_map/ppermute | solution.py:458
  13.3 23.0 %collective-permute-start.4 = (bf16[2,256,256]{2,1,0:T(8,128)(2,1)S(1)}, bf16[2,256,256]{2,1,0:T(8,128)(2,1)S(1)}, u32[]{:S(2)}, u32[]{:S(2)}) collective-permute-start(bf16[2,256,256]{2,1,0:T(8,128)(2,1)S(1)} %broadcast_select_fusion), channel_id=1, source_target_pairs={{0,1},{1,0},{2,3},{3,2},{4,5},{5,4},{6,7},{7,6},{8,9},{9,8},{10,11... | collective-permute-start | bytes 786440 | tf_op jit(solution)/shard_map/ppermute | solution.py:433
  14.9 21.9 %collective-permute-start.6 = (bf16[2,256,256]{2,1,0:T(8,128)(2,1)S(1)}, bf16[2,256,256]{2,1,0:T(8,128)(2,1)S(1)}, u32[]{:S(2)}, u32[]{:S(2)}) collective-permute-start(bf16[2,256,256]{2,1,0:T(8,128)(2,1)S(1)} %broadcast_select_fusion), channel_id=1, source_target_pairs={{1,2},{3,4},{5,6},{2,1},{4,3},{6,5},{9,10},{11,12},{13,14},{10,9},... | collective-permute-start | bytes 786440 | tf_op jit(solution)/shard_map/ppermute | solution.py:434
  21.4 22.6 %collective-permute-start.3 = (bf16[3,2,144,256]{3,2,1,0:T(8,128)(2,1)}, bf16[3,2,144,256]{3,2,1,0:T(8,128)(2,1)S(1)}, u32[]{:S(2)}, u32[]{:S(2)}) collective-permute-start(bf16[3,2,144,256]{3,2,1,0:T(8,128)(2,1)} %collective-permute-done.2.refs_5_), channel_id=1, source_target_pairs={{0,8},{8,0},{16,24},{24,16},{1,9},{9,1},{17,25},{25,17},{2,10},{10... | collective-permute-start | bytes 1327112 | tf_op jit(solution)/shard_map/ppermute | solution.py:459
  30.9 16.1 %collective-permute-start.9 = (bf16[3,2,144,256]{3,2,1,0:T(8,128)(2,1)}, bf16[3,2,144,256]{3,2,1,0:T(8,128)(2,1)S(1)}, u32[]{:S(2)}, u32[]{:S(2)}) collective-permute-start(bf16[3,2,144,256]{3,2,1,0:T(8,128)(2,1)} %collective-permute-done.8.refs_5_), channel_id=1, source_target_pairs={{0,8},{8,0},{16,24},{24,16},{1,9},{9,1},{17,25},{25,17},{2,10},{10... | collective-permute-start | bytes 1327112 | tf_op jit(solution)/shard_map/ppermute | solution.py:459
  36.3 4.1 %collective-permute-start.11 = (bf16[3,2,96,256]{3,2,1,0:T(8,128)(2,1)S(1)}, bf16[3,2,96,256]{3,2,1,0:T(8,128)(2,1)S(1)}, u32[]{:S(2)}, u32[]{:S(2)}) collective-permute-start(bf16[3,2,96,256]{3,2,1,0:T(8,128)(2,1)S(1)} %collective-permute-done.10.refs_5_), channel_id=1, source_target_pairs={{0,8},{8,0},{16,24},{24,16},{1,9},{9,1},{17,25},{25,17},{2,10},{10... | collective-permute-start | bytes 884744 | tf_op jit(solution)/shard_map/ppermute | solution.py:459
  36.3 2.0 %collective-permute-start.5 = (bf16[2,256,256]{2,1,0:T(8,128)(2,1)S(1)}, bf16[2,256,256]{2,1,0:T(8,128)(2,1)S(1)}, u32[]{:S(2)}, u32[]{:S(2)}) collective-permute-start(bf16[2,256,256]{2,1,0:T(8,128)(2,1)S(1)} %collective-permute-done.4.near), channel_id=1, source_target_pairs={{0,8},{8,0},{16,24},{24,16},{1,9},{9,1},{17,25},{25,17},{2,10},{10... | collective-permute-start | bytes 786440 | tf_op jit(solution)/shard_map/ppermute | solution.py:435
  36.8 1.8 %collective-permute-start.7 = (bf16[2,256,256]{2,1,0:T(8,128)(2,1)S(1)}, bf16[2,256,256]{2,1,0:T(8,128)(2,1)S(1)}, u32[]{:S(2)}, u32[]{:S(2)}) collective-permute-start(bf16[2,256,256]{2,1,0:T(8,128)(2,1)S(1)} %collective-permute-done.6.far), channel_id=1, source_target_pairs={{0,8},{8,0},{16,24},{24,16},{1,9},{9,1},{17,25},{25,17},{2,10},{10... | collective-permute-start | bytes 786440 | tf_op jit(solution)/shard_map/ppermute | solution.py:436
  39.5 0.9 %copy-start.4 = (bf16[1536,256]{1,0:T(8,128)(2,1)}, bf16[1536,256]{1,0:T(8,128)(2,1)S(1)}, u32[]{:S(2)}) copy-start(bf16[1536,256]{1,0:T(8,128)(2,1)S(1)} %get-tuple-element.19.refs_8_) | copy-start | bytes 2359300
  42.4 15.4 %collective-permute-start.14 = (bf16[2,2,64,256]{3,2,1,0:T(8,128)(2,1)S(1)}, bf16[2,2,64,256]{3,2,1,0:T(8,128)(2,1)S(1)}, u32[]{:S(2)}, u32[]{:S(2)}) collective-permute-start(bf16[2,2,64,256]{3,2,1,0:T(8,128)(2,1)S(1)} %get-tuple-element.27), channel_id=1, source_target_pairs={{0,1},{1,0},{2,3},{3,2},{4,5},{5,4},{6,7},{7,6},{8,9},{9,8},{10,11... | collective-permute-start | bytes 393224 | tf_op jit(solution)/shard_map/ppermute | solution.py:472
  46.5 20.6 %collective-permute-start.12 = (bf16[2,2,96,256]{3,2,1,0:T(8,128)(2,1)S(1)}, bf16[2,2,96,256]{3,2,1,0:T(8,128)(2,1)S(1)}, u32[]{:S(2)}, u32[]{:S(2)}) collective-permute-start(bf16[2,2,96,256]{3,2,1,0:T(8,128)(2,1)S(1)} %get-tuple-element.25), channel_id=1, source_target_pairs={{0,1},{1,0},{2,3},{3,2},{4,5},{5,4},{6,7},{7,6},{8,9},{9,8},{10,11... | collective-permute-start | bytes 589832 | tf_op jit(solution)/shard_map/ppermute | solution.py:472
  49.5 19.1 %collective-permute-start.13 = (bf16[2,2,96,256]{3,2,1,0:T(8,128)(2,1)S(1)}, bf16[2,2,96,256]{3,2,1,0:T(8,128)(2,1)S(1)}, u32[]{:S(2)}, u32[]{:S(2)}) collective-permute-start(bf16[2,2,96,256]{3,2,1,0:T(8,128)(2,1)S(1)} %get-tuple-element.26), channel_id=1, source_target_pairs={{0,1},{1,0},{2,3},{3,2},{4,5},{5,4},{6,7},{7,6},{8,9},{9,8},{10,11... | collective-permute-start | bytes 589832 | tf_op jit(solution)/shard_map/ppermute | solution.py:472
  51.1 17.6 %collective-permute-start.15 = (bf16[2,2,96,256]{3,2,1,0:T(8,128)(2,1)S(1)}, bf16[2,2,96,256]{3,2,1,0:T(8,128)(2,1)S(1)}, u32[]{:S(2)}, u32[]{:S(2)}) collective-permute-start(bf16[2,2,96,256]{3,2,1,0:T(8,128)(2,1)S(1)} %get-tuple-element.28), channel_id=1, source_target_pairs={{1,2},{3,4},{5,6},{2,1},{4,3},{6,5},{9,10},{11,12},{13,14},{10,9},... | collective-permute-start | bytes 589832 | tf_op jit(solution)/shard_map/ppermute | solution.py:473
  53.4 15.3 %collective-permute-start.16 = (bf16[2,2,96,256]{3,2,1,0:T(8,128)(2,1)S(1)}, bf16[2,2,96,256]{3,2,1,0:T(8,128)(2,1)S(1)}, u32[]{:S(2)}, u32[]{:S(2)}) collective-permute-start(bf16[2,2,96,256]{3,2,1,0:T(8,128)(2,1)S(1)} %get-tuple-element.29), channel_id=1, source_target_pairs={{1,2},{3,4},{5,6},{2,1},{4,3},{6,5},{9,10},{11,12},{13,14},{10,9},... | collective-permute-start | bytes 589832 | tf_op jit(solution)/shard_map/ppermute | solution.py:473
  57.8 9.2 %collective-permute-start.17 = (bf16[2,2,64,256]{3,2,1,0:T(8,128)(2,1)S(1)}, bf16[2,2,64,256]{3,2,1,0:T(8,128)(2,1)S(1)}, u32[]{:S(2)}, u32[]{:S(2)}) collective-permute-start(bf16[2,2,64,256]{3,2,1,0:T(8,128)(2,1)S(1)} %get-tuple-element.30), channel_id=1, source_target_pairs={{1,2},{3,4},{5,6},{2,1},{4,3},{6,5},{9,10},{11,12},{13,14},{10,9},... | collective-permute-start | bytes 393224 | tf_op jit(solution)/shard_map/ppermute | solution.py:473
